TPU v7x, 32 devices: a whole 2x2x4 slice. The times are simulated.
32 devices in a mesh: dp: 4 (over y, x), seq: 4 (over z), head: 2 (over core).
Axes of the slice: x: 2, y: 2, z: 4, core: 2. Of those that a mesh axis runs over, the one named last changes fastest.
Arguments:
- latents: bfloat16 [4, 1024, 2048], P('dp', 'seq'), may hold values from -6 to 6
- w_qkv: bfloat16 [2048, 3, 1536], P(None, None, 'head'), may hold values from -0.125 to 0.125
- q_gain: float32 [128], replicated, may hold values from 0.1 to 1.9
- k_gain: float32 [128], replicated, may hold values from 0.1 to 1.9
- neighbours: int32 [16, 9], replicated, may hold values from -1 to 15, as said below
- grad_out: bfloat16 [4, 1024, 1536], P('dp', 'seq', 'head'), may hold values from -6 to 6
Outputs:
- attn_out: bfloat16 [4, 1024, 1536], P('dp', 'seq', 'head')
- grad_x: bfloat16 [4, 1024, 2048], P('dp', ('seq', 'head'))
- grad_w: float32 [2048, 3, 1536], P(('dp', 'seq'), None, 'head')
Inputs may be any that keep to these rules, and one draw needn't show every extreme that they name: `neighbours`: row t lists only tiles whose slab differs from that of t (t // 4) by at most one and whose position in the slab (index % 4) differs by at most one, each at most once; t itself is always listed.
All inputs are finite; a program needn't handle non-finite values.
Results may differ from a plain program's by a relative error of at most 0.017.
Values may be sent and summed in bfloat16 or wider, within the bound.
A program may use at most 128 MiB of HBM per device.

v0:
```python
import math

import jax
import jax.numpy as jnp
from jax import lax
from jax.sharding import PartitionSpec as P

HD = 128
TILE = 64


EPS = 1e-06


def with_halo(block, sides, width):
    for axis, dim in sides:
        count = lax.axis_size(axis)
        forward = [(i, i + 1) for i in range(count - 1)]
        backward = [(target, source) for source, target in forward]
        low = lax.ppermute(
            lax.slice_in_dim(block, block.shape[dim] - width, None, axis=dim), axis, forward
        )
        high = lax.ppermute(lax.slice_in_dim(block, 0, width, axis=dim), axis, backward)
        block = jnp.concatenate([low, block, high], axis=dim)
    return block


def inv_rms(values):
    return lax.rsqrt(jnp.mean(values * values, axis=-1, keepdims=True) + EPS)


def norm_back(raw, inverse, gain, upstream):
    normed = raw * inverse
    weighted = upstream * gain
    return inverse * (weighted - normed * jnp.mean(weighted * normed, axis=-1, keepdims=True))


def tile_allowed(neighbours, query_first, query_count, key_first, key_count):
    tile_total = neighbours.shape[0]
    padded = jnp.pad(neighbours, ((query_count, query_count), (0, 0)), constant_values=-1)
    picked = lax.dynamic_slice_in_dim(padded, query_first + query_count, query_count, 0)
    query_ids = query_first + jnp.arange(query_count, dtype=jnp.int32)
    key_ids = key_first + jnp.arange(key_count, dtype=jnp.int32)
    query_valid = (query_ids >= 0) & (query_ids < tile_total)
    key_valid = (key_ids >= 0) & (key_ids < tile_total)
    hits = jnp.any(picked[:, :, None] == key_ids[None, None, :], axis=1)
    hits = hits & query_valid[:, None] & key_valid[None, :]
    block = jnp.where(hits, 1.0, 0.0).astype(jnp.float32)
    return jnp.repeat(jnp.repeat(block, TILE, axis=0), TILE, axis=1)


def local(latents, w_qkv, q_gain, k_gain, neighbours, grad_out):
    slab_tokens = latents[0]
    slab_rows = slab_tokens.shape[0]
    model_width = w_qkv.shape[0]
    head_width = w_qkv.shape[2]
    head_count = head_width // HD
    tiles_slab = slab_rows // TILE
    score_scale = 1.0 / math.sqrt(HD)
    flat_w = w_qkv.reshape(model_width, 3 * head_width)
    qkv = jnp.dot(slab_tokens, flat_w, preferred_element_type=jnp.float32).reshape(
        slab_rows, 3, head_count, HD
    )
    q_raw = qkv[:, 0]
    k_raw = qkv[:, 1]
    v_raw = qkv[:, 2]
    q_inv = inv_rms(q_raw)
    k_inv = inv_rms(k_raw)
    q_hat = (q_raw * q_inv * q_gain).astype(jnp.bfloat16)
    k_hat = (k_raw * k_inv * k_gain).astype(jnp.bfloat16)
    v_hat = v_raw.astype(jnp.bfloat16)
    stacked = jnp.stack(
        [k_hat.reshape(slab_rows, head_width), v_hat.reshape(slab_rows, head_width)], axis=1
    )
    widened = with_halo(stacked, (("seq", 0),), slab_rows)
    keys_wide = widened[:, 0].reshape(3 * slab_rows, head_count, HD)
    values_wide = widened[:, 1].reshape(3 * slab_rows, head_count, HD)
    seq_slab = lax.axis_index("seq")
    own_tile = seq_slab * tiles_slab
    first_tile = (seq_slab - 1) * tiles_slab
    allowed = tile_allowed(neighbours, own_tile, tiles_slab, first_tile, 3 * tiles_slab)
    scores = (
        jnp.einsum("qhe,khe->hqk", q_hat, keys_wide, preferred_element_type=jnp.float32)
        * score_scale
    )
    exponent = jnp.exp(scores) * allowed[None]
    row_total = jnp.sum(exponent, axis=-1)
    probs = exponent / row_total[..., None]
    probs_b = probs.astype(jnp.bfloat16)
    attended = jnp.einsum("hqk,khe->qhe", probs_b, values_wide, preferred_element_type=jnp.float32)
    attn_out = attended.astype(jnp.bfloat16).reshape(1, slab_rows, head_width)
    upstream = grad_out[0].reshape(slab_rows, head_count, HD)
    d_probs = jnp.einsum("qhe,khe->hqk", upstream, values_wide, preferred_element_type=jnp.float32)
    row_delta = jnp.sum(probs * d_probs, axis=-1)
    d_scores = (probs * (d_probs - row_delta[..., None]) * score_scale).astype(jnp.bfloat16)
    d_qhat = jnp.einsum("hqk,khe->qhe", d_scores, keys_wide, preferred_element_type=jnp.float32)
    query_pack = jnp.stack([q_hat.reshape(slab_rows, head_width), grad_out[0]], axis=1)
    row_stats = jnp.transpose(jnp.stack([row_total, row_delta], axis=0), (2, 0, 1))
    pack_wide = with_halo(query_pack, (("seq", 0),), slab_rows)
    stats_wide = with_halo(row_stats, (("seq", 0),), slab_rows)
    queries_wide = pack_wide[:, 0].reshape(3 * slab_rows, head_count, HD)
    upstream_wide = pack_wide[:, 1].reshape(3 * slab_rows, head_count, HD)
    total_wide = jnp.transpose(stats_wide[:, 0])
    delta_wide = jnp.transpose(stats_wide[:, 1])
    safe_total = jnp.where(total_wide > 0.0, total_wide, 1.0)
    reverse_allowed = tile_allowed(neighbours, first_tile, 3 * tiles_slab, own_tile, tiles_slab)
    scores_back = (
        jnp.einsum("qhe,khe->hqk", queries_wide, k_hat, preferred_element_type=jnp.float32)
        * score_scale
    )
    probs_back = jnp.exp(scores_back) * reverse_allowed[None] / safe_total[..., None]
    probs_back_b = probs_back.astype(jnp.bfloat16)
    d_probs_back = jnp.einsum(
        "qhe,khe->hqk", upstream_wide, v_hat, preferred_element_type=jnp.float32
    )
    d_scores_back = (probs_back * (d_probs_back - delta_wide[..., None]) * score_scale).astype(
        jnp.bfloat16
    )
    d_khat = jnp.einsum(
        "hqk,qhe->khe", d_scores_back, queries_wide, preferred_element_type=jnp.float32
    )
    d_value = jnp.einsum(
        "hqk,qhe->khe", probs_back_b, upstream_wide, preferred_element_type=jnp.float32
    )
    d_query = norm_back(q_raw, q_inv, q_gain, d_qhat)
    d_key = norm_back(k_raw, k_inv, k_gain, d_khat)
    d_qkv = (
        jnp.stack([d_query, d_key, d_value], axis=1)
        .astype(jnp.bfloat16)
        .reshape(slab_rows, 3 * head_width)
    )
    grad_rows = lax.psum_scatter(
        lax.dot_general(
            d_qkv, flat_w, (((1,), (1,)), ((), ())), preferred_element_type=jnp.float32
        ),
        "head",
        scatter_dimension=0,
        tiled=True,
    )
    grad_x = grad_rows.astype(jnp.bfloat16)[None]
    product = lax.dot_general(
        slab_tokens, d_qkv, (((0,), (0,)), ((), ())), preferred_element_type=jnp.float32
    )
    clip_share = lax.psum_scatter(
        product.reshape(
            model_width // lax.axis_size("dp") * lax.axis_size("dp"), 3, head_width
        ).astype(jnp.bfloat16),
        "dp",
        scatter_dimension=0,
        tiled=True,
    )
    grad_w = lax.psum_scatter(clip_share, "seq", scatter_dimension=0, tiled=True).astype(
        jnp.float32
    )
    return (attn_out, grad_x, grad_w)


def solution(mesh):
    in_specs = (P("dp", "seq", None), P(None, None, "head"), P(), P(), P(), P("dp", "seq", "head"))
    out_specs = (
        P("dp", "seq", "head"),
        P("dp", ("seq", "head"), None),
        P(("dp", "seq"), None, "head"),
    )
    return jax.shard_map(local, mesh=mesh, in_specs=in_specs, out_specs=out_specs, check_vma=False)
```

profile of v0, /device:TPU:0, one launch (start us, length us, event | category | flops | bytes accessed | tf_op | source)
XLA Modules:
  0.0 275.9 jit_solution(8086367946032504277)
XLA Ops:
  7.2 0.0 copy-start
  7.2 0.0 reduce-scatter.6.cloned.1.call-start
  7.2 12.6 %copy.67 = bf16[2048,3,768]{0,2,1:T(8,128)(2,1)} copy(bf16[2048,3,768]{2,0,1:T(8,128)(2,1)} %param.7) | data formatting | bytes 18874368 | tf_op args[1]
  19.8 5.2 %fusion.36 = f32[256,3,6,128]{0,3,2,1:T(8,128)S(1)} fusion(bf16[3,6,128,2048]{3,2,1,0:T(8,128)(2,1)} %bitcast.149, bf16[1,256,2048]{2,1,0:T(8,128)(2,1)S(1)} %copy-done), kind=kOutput, calls=%fused_computation.33 | convolution fusion | flops 2415919104 | bytes 12845056 | tf_op jit(solution)/shard_map/dot_general | solution.py:61
  25.1 0.1 fusion.41
  25.3 1.0 fusion.61
  26.4 0.1 mul.202
  26.4 0.2 fusion.43
  26.6 1.0 pad_maximum_fusion.3
  27.6 1.3 collective-permute-start.1
  28.9 6.5 %collective-permute-start = (bf16[256,2,768]{0,2,1:T(8,128)(2,1)}, bf16[256,2,768]{0,2,1:T(8,128)(2,1)}, u32[]{:S(2)}, u32[]{:S(2)}) collective-permute-start(bf16[256,2,768]{0,2,1:T(8,128)(2,1)} %pad_maximum_fusion.3), channel_id=1, source_target_pairs={{0,2},{2,4},{4,6},{1,3},{3,5},{5,7},{8,10},{10,12},{12,14},{9,11},... | collective-permute-start | bytes 2359304 | tf_op jit(solution)/shard_map/ppermute | solution.py:20
  35.4 1.9 copy.73
  37.3 0.1 mul.210
  37.4 1.3 fusion.40
  38.7 0.7 copy-done.8
  39.4 2.0 pad_maximum_fusion.4
  41.4 1.3 collective-permute-start.3
  42.7 5.5 %collective-permute-start.2 = (bf16[256,2,768]{0,2,1:T(8,128)(2,1)}, bf16[256,2,768]{0,2,1:T(8,128)(2,1)}, u32[]{:S(2)}, u32[]{:S(2)}) collective-permute-start(bf16[256,2,768]{0,2,1:T(8,128)(2,1)} %pad_maximum_fusion.4), channel_id=1, source_target_pairs={{0,2},{2,4},{4,6},{1,3},{3,5},{5,7},{8,10},{10,12},{12,14},{9,11},... | collective-permute-start | bytes 2359304 | tf_op jit(solution)/shard_map/ppermute | solution.py:20
  48.2 0.1 copy.70
  48.3 0.1 compare_reduce_fusion.1
  48.4 0.1 and_select_fusion.1
  48.5 0.1 copy.71
  48.6 0.1 copy.80
  48.7 0.1 broadcast_in_dim.32
  48.7 0.1 reshape.212
  48.8 0.1 compare_reduce_fusion
  48.9 0.1 and_select_fusion
  49.0 0.1 broadcast_in_dim.61
  49.1 0.1 reshape.214
  49.2 0.9 broadcast_in_dim.33
  50.1 2.3 copy.72
  52.4 0.9 broadcast_in_dim.62
  53.4 2.3 copy.81
  55.7 1.8 pad_maximum_fusion
  57.5 0.2 fusion.62
  57.7 1.0 copy-done.5
  58.7 1.5 fusion.5
  60.2 3.6 %fusion = (f32[6,256]{1,0:T(8,128)S(1)}, f32[6,768,256]{1,2,0:T(8,128)}) fusion(f32[6,256]{1,0:T(8,128)S(1)} %get-tuple-element.30, f32[256,768]{1,0:T(8,128)S(1)} %copy-done.12, f32[6,256,768]{2,1,0:T(8,128)S(1)} %get-tuple-element.31, bf16[768,6,128]{0,2,1:T(8,128)(2,1)S(1)} %bitcast.169, bf16[256,6,128]{0,2,1:T(8,128)(2,1)S(1)} %bitcast.161), kind=kOutput, calls=%fused_computation.3 | convolution fusion | flops 307886592 | bytes 11808768 | tf_op jit(solution)/shard_map/qhe,khe->hqk/dot_general | solution.py:93
  63.8 1.4 collective-permute-start.5
  65.3 4.7 %collective-permute-start.4 = (f32[256,2,6]{0,2,1:T(8,128)S(1)}, f32[256,2,6]{0,2,1:T(8,128)S(1)}, u32[]{:S(2)}, u32[]{:S(2)}) collective-permute-start(f32[256,2,6]{0,2,1:T(8,128)S(1)} %maximum_bitcast_fusion), channel_id=1, source_target_pairs={{0,2},{2,4},{4,6},{1,3},{3,5},{5,7},{8,10},{10,12},{12,14},{9,11},... | collective-permute-start | bytes 36872 | tf_op jit(solution)/shard_map/ppermute | solution.py:20
  70.0 1.5 pad_maximum_fusion.1
  71.6 0.2 fusion.60
  71.8 1.8 multiply_divide_fusion
  73.6 2.1 copy-done.1
  75.7 1.2 fusion.33
  77.0 5.3 %fusion.26 = f32[256,6,128]{0,2,1:T(8,128)} fusion(bf16[768,6,128]{0,2,1:T(8,128)(2,1)} %bitcast.157, f32[6,768,256]{2,1,0:T(8,128)} %copy-done.1, bf16[768,6,128]{0,2,1:T(8,128)(2,1)} %bitcast.155, f32[6,768]{1,0:T(8,128)S(1)} %slice_bitcast_fusion, f32[128]{0:T(128)S(1)} %copy-done.18, f32[256,3,6,128]{0,3,2,1:T(8,128)S(1)} %fusion.36), kind=kOutput, calls=%fused_computation.28 | convolution fusion | flops 608894976 | bytes 8282624 | tf_op jit(solution)/shard_map/hqk,qhe->khe/dot_general | solution.py:119
  82.3 6.4 %multiply_reduce_fusion.1 = (f32[256,6]{0,1:T(8,128)S(1)}, f32[256,6]{0,1:T(8,128)S(1)}, f32[256,6,128]{0,2,1:T(8,128)S(1)}) fusion(f32[256,6]{0,1:T(8,128)S(1)} %get-tuple-element.35, f32[256,3,6,128]{0,3,2,1:T(8,128)S(1)} %fusion.36, f32[256,6,128]{0,2,1:T(8,128)} %fusion.26, f32[256,6]{0,1:T(8,128)S(1)} %get-tuple-element.36, f32[128]{0:T(128)S(1)} %copy-done.19, ...), kind=kOutput, calls=%fused_computation.55 | convolution fusion | flops 311620608 | bytes 14586368 | tf_op jit(solution)/shard_map/hqk,khe->qhe/dot_general | solution.py:96
  88.7 0.4 fusion.46
  89.1 0.1 pad_maximum_fusion.2
  89.2 5.1 %convolution_convert_fusion = bf16[2304,2048]{1,0:T(8,128)(2,1)} fusion(bf16[256,2304]{0,1:T(8,128)(2,1)S(1)} %bitcast.152, bf16[1,256,2048]{2,1,0:T(8,128)(2,1)S(1)} %copy-done), kind=kOutput, calls=%fused_computation | convolution fusion | flops 2420637696 | bytes 11665408 | tf_op jit(solution)/shard_map/dot_general | solution.py:141
  94.3 12.6 %copy.84 = bf16[2048,3,768]{2,0,1:T(8,128)(2,1)} copy(bf16[2048,3,768]{0,2,1:T(8,128)(2,1)} %bitcast.151) | data formatting | bytes 18874368 | tf_op jit(solution)/shard_map/convert_element_type | solution.py:147
  107.0 0.0 reduce-scatter.6.cloned.1.call-update
  107.0 0.0 reduce-scatter.4.cloned.1.call-start
  107.0 7.7 %fusion.65 = f32[256,2048]{1,0:T(8,128)} fusion(bf16[256,2304]{0,1:T(8,128)(2,1)S(1)} %bitcast.153, bf16[2048,2304]{0,1:T(8,128)(2,1)} %bitcast.150), kind=kOutput, calls=%fused_computation.95 | convolution fusion | flops 2415919104 | bytes 12713984 | tf_op jit(solution)/shard_map/dot_general | solution.py:133
  114.8 0.0 reduce-scatter.4.cloned.1.call-update
  114.8 0.0 reduce-scatter.8.cloned.1.call-start
  114.8 89.1 %reduce-scatter.6.cloned.1.call-done = bf16[512,3,768]{2,0,1:T(8,128)(2,1)} async-done(((bf16[2048,3,768]{2,0,1:T(8,128)(2,1)}), bf16[512,3,768]{2,0,1:T(8,128)(2,1)}) %reduce-scatter.6.cloned.1.call-update) | async-done | bytes 2359312 | tf_op jit(solution)/shard_map/reduce_scatter | solution.py:144
  203.9 0.0 reduce-scatter.8.cloned.1.call-update
  203.9 3.9 %fusion.27 = bf16[6,128,256]{2,1,0:T(8,128)(2,1)S(1)} fusion(bf16[768,6,128]{0,2,1:T(8,128)(2,1)} %bitcast.170, f32[6,256,768]{2,1,0:T(8,128)} %copy-done.4, f32[6,256]{1,0:T(8,128)S(1)} %get-tuple-element.30, f32[256,768]{1,0:T(8,128)S(1)} %copy-done.13), kind=kOutput, calls=%fused_computation.29 | convolution fusion | flops 306905088 | bytes 7084032 | tf_op jit(solution)/shard_map/hqk,khe->qhe/dot_general | solution.py:90
  207.9 0.9 copy.85
  208.8 7.1 %reduce-scatter.4.cloned.1.call-done = f32[128,2048]{1,0:T(8,128)} async-done(((f32[256,2048]{1,0:T(8,128)}), f32[128,2048]{1,0:T(8,128)}) %reduce-scatter.4.cloned.1.call-update) | async-done | bytes 1048592 | tf_op jit(solution)/shard_map/reduce_scatter | solution.py:132
  215.9 2.1 convert_bitcast_fusion
  218.0 49.2 %reduce-scatter.8.cloned.1.call-done = bf16[128,3,768]{2,0,1:T(8,128)(2,1)} async-done(((bf16[512,3,768]{2,0,1:T(8,128)(2,1)}), bf16[128,3,768]{2,0,1:T(8,128)(2,1)}) %reduce-scatter.8.cloned.1.call-update) | async-done | bytes 589840 | tf_op jit(solution)/shard_map/reduce_scatter | solution.py:152
  267.2 2.2 convert_element_type.106
  (58 shorter events, 0.2 us)
Async XLA Ops:
  7.2 12.7 %copy-start = (bf16[1,256,2048]{2,1,0:T(8,128)(2,1)S(1)}, bf16[1,256,2048]{2,1,0:T(8,128)(2,1)}, u32[]{:S(2)}) copy-start(bf16[1,256,2048]{2,1,0:T(8,128)(2,1)} %param.6) | copy-start | bytes 3145732
  7.2 196.7 %reduce-scatter.6.cloned.1.call-start = ((), (), s32[]{:S(2)}) async-start(), calls=%async_computation.4 | async-start | bytes 11796480 | tf_op jit(solution)/shard_map/reduce_scatter | solution.py:144
  25.1 1.3 copy-start.18
  25.1 10.3 %copy-start.19 = (f32[128]{0:T(128)S(1)}, f32[128]{0:T(128)}, u32[]{:S(2)}) copy-start(f32[128]{0:T(128)} %param.8) | copy-start | bytes 1540
  25.3 1.3 copy-start.7
  26.3 21.8 %copy-start.17 = (s32[16,9]{1,0:T(8,128)S(1)}, s32[16,9]{1,0:T(8,128)}, u32[]{:S(2)}) copy-start(s32[16,9]{1,0:T(8,128)} %param.10) | copy-start | bytes 1732
  26.6 1.0 copy-start.10
  27.6 28.0 %collective-permute-start.1 = (bf16[256,2,768]{0,2,1:T(8,128)(2,1)}, bf16[256,2,768]{0,2,1:T(8,128)(2,1)}, u32[]{:S(2)}, u32[]{:S(2)}) collective-permute-start(bf16[256,2,768]{0,2,1:T(8,128)(2,1)} %pad_maximum_fusion.3), channel_id=1, source_target_pairs={{2,0},{4,2},{6,4},{3,1},{5,3},{7,5},{10,8},{12,10},{14,12},{11,9},... | collective-permute-start | bytes 2359304 | tf_op jit(solution)/shard_map/ppermute | solution.py:23
  28.9 26.7 %collective-permute-start = (bf16[256,2,768]{0,2,1:T(8,128)(2,1)}, bf16[256,2,768]{0,2,1:T(8,128)(2,1)}, u32[]{:S(2)}, u32[]{:S(2)}) collective-permute-start(bf16[256,2,768]{0,2,1:T(8,128)(2,1)} %pad_maximum_fusion.3), channel_id=1, source_target_pairs={{0,2},{2,4},{4,6},{1,3},{3,5},{5,7},{8,10},{10,12},{12,14},{9,11},... | collective-permute-start | bytes 2359304 | tf_op jit(solution)/shard_map/ppermute | solution.py:20
  38.7 0.7 copy-start.8
  41.4 28.6 %collective-permute-start.3 = (bf16[256,2,768]{0,2,1:T(8,128)(2,1)}, bf16[256,2,768]{0,2,1:T(8,128)(2,1)}, u32[]{:S(2)}, u32[]{:S(2)}) collective-permute-start(bf16[256,2,768]{0,2,1:T(8,128)(2,1)} %pad_maximum_fusion.4), channel_id=1, source_target_pairs={{2,0},{4,2},{6,4},{3,1},{5,3},{7,5},{10,8},{12,10},{14,12},{11,9},... | collective-permute-start | bytes 2359304 | tf_op jit(solution)/shard_map/ppermute | solution.py:23
  42.7 27.4 %collective-permute-start.2 = (bf16[256,2,768]{0,2,1:T(8,128)(2,1)}, bf16[256,2,768]{0,2,1:T(8,128)(2,1)}, u32[]{:S(2)}, u32[]{:S(2)}) collective-permute-start(bf16[256,2,768]{0,2,1:T(8,128)(2,1)} %pad_maximum_fusion.4), channel_id=1, source_target_pairs={{0,2},{2,4},{4,6},{1,3},{3,5},{5,7},{8,10},{10,12},{12,14},{9,11},... | collective-permute-start | bytes 2359304 | tf_op jit(solution)/shard_map/ppermute | solution.py:20
  55.6 3.0 %copy-start.12 = (f32[256,768]{1,0:T(8,128)S(1)}, f32[256,768]{1,0:T(8,128)}, u32[]{:S(2)}) copy-start(f32[256,768]{1,0:T(8,128)} %copy.72) | copy-start | bytes 2359300
  57.7 1.0 copy-start.5
  57.7 6.2 %copy-start.15 = (bf16[768,1,768]{0,2,1:T(8,128)(2,1)}, bf16[768,1,768]{0,2,1:T(8,128)(2,1)S(1)}, u32[]{:S(2)}) copy-start(bf16[768,1,768]{0,2,1:T(8,128)(2,1)S(1)} %get-tuple-element.29) | copy-start | bytes 3538948
  57.7 2.5 copy-start.6
  60.2 3.7 %copy-start.4 = (f32[6,256,768]{2,1,0:T(8,128)}, f32[6,256,768]{2,1,0:T(8,128)S(1)}, u32[]{:S(2)}) copy-start(f32[6,256,768]{2,1,0:T(8,128)S(1)} %get-tuple-element.31) | copy-start | bytes 14155780
  60.2 9.9 %copy-start.9 = (bf16[256,1,768]{0,2,1:T(8,128)(2,1)S(1)}, bf16[256,1,768]{0,2,1:T(8,128)(2,1)}, u32[]{:S(2)}) copy-start(bf16[256,1,768]{0,2,1:T(8,128)(2,1)} %copy-done.8) | copy-start | bytes 1179652
  63.8 8.0 %copy-start.16 = (f32[768,256]{1,0:T(8,128)S(1)}, f32[768,256]{1,0:T(8,128)}, u32[]{:S(2)}) copy-start(f32[768,256]{1,0:T(8,128)} %copy.81) | copy-start | bytes 2359300
  63.8 7.9 %collective-permute-start.5 = (f32[256,2,6]{0,2,1:T(8,128)S(1)}, f32[256,2,6]{0,2,1:T(8,128)S(1)}, u32[]{:S(2)}, u32[]{:S(2)}) collective-permute-start(f32[256,2,6]{0,2,1:T(8,128)S(1)} %maximum_bitcast_fusion), channel_id=1, source_target_pairs={{2,0},{4,2},{6,4},{3,1},{5,3},{7,5},{10,8},{12,10},{14,12},{11,9},... | collective-permute-start | bytes 36872 | tf_op jit(solution)/shard_map/ppermute | solution.py:23
  65.3 6.5 %collective-permute-start.4 = (f32[256,2,6]{0,2,1:T(8,128)S(1)}, f32[256,2,6]{0,2,1:T(8,128)S(1)}, u32[]{:S(2)}, u32[]{:S(2)}) collective-permute-start(f32[256,2,6]{0,2,1:T(8,128)S(1)} %maximum_bitcast_fusion), channel_id=1, source_target_pairs={{0,2},{2,4},{4,6},{1,3},{3,5},{5,7},{8,10},{10,12},{12,14},{9,11},... | collective-permute-start | bytes 36872 | tf_op jit(solution)/shard_map/ppermute | solution.py:20
  71.7 1.9 copy-start.3
  71.7 1.9 copy-start.2
  73.6 2.1 copy-start.1
  82.3 6.4 %copy-start.11 = (f32[256,6,128]{0,2,1:T(8,128)S(1)}, f32[256,6,128]{0,2,1:T(8,128)}, u32[]{:S(2)}) copy-start(f32[256,6,128]{0,2,1:T(8,128)} %fusion.26) | copy-start | bytes 2359300
  82.3 6.8 %copy-start.14 = (bf16[256,1,6,128]{0,3,2,1:T(8,128)(2,1)S(1)}, bf16[256,1,6,128]{0,3,2,1:T(8,128)(2,1)}, u32[]{:S(2)}) copy-start(bf16[256,1,6,128]{0,3,2,1:T(8,128)(2,1)} %fusion.33) | copy-start | bytes 1179652
  107.0 108.9 %reduce-scatter.4.cloned.1.call-start = ((), (), s32[]{:S(2)}) async-start(), calls=%async_computation.3 | async-start | bytes 3145728 | tf_op jit(solution)/shard_map/reduce_scatter | solution.py:132
  107.0 96.9 %copy-start.13 = (f32[256,768]{1,0:T(8,128)S(1)}, f32[256,768]{1,0:T(8,128)}, u32[]{:S(2)}) copy-start(f32[256,768]{1,0:T(8,128)} %copy.72) | copy-start | bytes 2359300
  114.8 152.5 %reduce-scatter.8.cloned.1.call-start = ((), (), s32[]{:S(2)}) async-start(), calls=%async_computation.5 | async-start | bytes 2949120 | tf_op jit(solution)/shard_map/reduce_scatter | solution.py:152
Sparse Core Ops, SparseCore 0:
  107.1 96.7 reduce-scatter.5
  206.1 9.7 reduce-scatter.3
  218.2 48.9 reduce-scatter.7
where the time goes:
time: 277 us; the launch traced here: 276 us
  waiting for transfers between devices  145 us (52%)
  matrix products  41.8 us (15%)
  local copies, waits for them, and re-layouts  40.6 us (15%)
  starting transfers between devices  20.8 us (8%)
  between operations  14.2 us (5%)
  other arithmetic  13.1 us (5%)
    reduce_scatter x1, waiting for transfers between devices, local(): lax.psum_scatter(product.reshape(model_width // lax.axis_size('dp') * lax...  89.1 us
    reduce_scatter x1, waiting for transfers between devices, local(): lax.psum_scatter(clip_share, 'seq', scatter_dimension=0, tiled=True)  49.2 us
    unnamed x43, local copies, waits for them, and re-layouts  19.4 us
    ppermute x3, starting transfers between devices, with_halo(): lax.ppermute(lax.slice_in_dim(block, block.shape[dim] - width, None, axis...  16.7 us
    convert_element_type x1, local copies, waits for them, and re-layouts, local(): clip_share = lax.psum_scatter(product.reshape(model_width // lax.axis_siz...  12.6 us
    dot_general x1, matrix products, local(): lax.dot_general(d_qkv, flat_w, (((1,), (1,)), ((), ())), preferred_elemen...  7.72 us
    reduce_scatter x1, waiting for transfers between devices, local(): lax.psum_scatter(lax.dot_general(d_qkv, flat_w, (((1,), (1,)), ((), ())),...  7.12 us
    dot_general x1, matrix products, local(): jnp.einsum('hqk,khe->qhe', d_scores, keys_wide, preferred_element_type=jn...  6.36 us
  transfers between devices with their start and end apart: 9, of which 3 were waited for; matrix products, arithmetic and copies ran while one was open for 13% of the time, Pallas kernels for 0%

commit v1 on v0

--- a/solution.py
+++ b/solution.py
@@ -1,9 +1,14 @@
+import functools
 import math
 
 import jax
 import jax.numpy as jnp
 from jax import lax
+from jax.experimental import pallas as pl
+from jax.experimental.pallas import tpu as pltpu
 from jax.sharding import PartitionSpec as P
+
+MESH = pl.DeviceIdType.MESH
 
 HD = 128
 TILE = 64
@@ -47,6 +52,230 @@
     hits = hits & query_valid[:, None] & key_valid[None, :]
     block = jnp.where(hits, 1.0, 0.0).astype(jnp.float32)
     return jnp.repeat(jnp.repeat(block, TILE, axis=0), TILE, axis=1)
+
+
+def remote(src, dst, send_sem, recv_sem, peer):
+    return pltpu.make_async_remote_copy(
+        src_ref=src,
+        dst_ref=dst,
+        send_sem=send_sem,
+        recv_sem=recv_sem,
+        device_id=peer,
+        device_id_type=MESH,
+    )
+
+
+def grads_kernel(
+    n_dp, n_seq, n_head, dq_ref, lat_ref, w_ref, gw_ref, gx_ref,
+    gath, w_buf, part, z_send, z_recv, gx_acc, gx_recv,
+    w_sem, d_ss, d_rs, z_ss, z_rs, h_ss, h_rs,
+):
+    chunks, slab, width = dq_ref.shape
+    rows = part.shape[1]
+    half = gx_ref.shape[0]
+    me_dp = lax.axis_index("dp")
+    me_seq = lax.axis_index("seq")
+    me_head = lax.axis_index("head")
+    relay = n_dp == 4
+
+    def dp_peer(step):
+        if relay:
+            low, high = lax.rem(me_dp, 2), me_dp // 2
+            if step % 2:
+                low = 1 - low
+            if step // 2:
+                high = 1 - high
+            return {"dp": high * 2 + low}
+        return {"dp": lax.rem(me_dp + step, n_dp)}
+
+    def dp_source(step):
+        if relay:
+            return dp_peer(step)
+        return {"dp": lax.rem(me_dp + n_dp - step, n_dp)}
+
+    direct = (1, 2) if relay else tuple(range(1, n_dp))
+
+    def seq_peer(step):
+        return lax.rem(me_seq + step, n_seq)
+
+    def head_peer(step):
+        return lax.rem(me_head + step, n_head)
+
+    def w_copy(c):
+        return pltpu.make_async_copy(
+            w_ref.at[:, pl.ds(pl.multiple_of(c * width, width), width)],
+            w_buf.at[c],
+            w_sem.at[c],
+        )
+
+    @pl.loop(0, chunks)
+    def _(c):
+        w_copy(c).start()
+
+    barrier = pltpu.get_barrier_semaphore()
+    greeted = 0
+    for step in direct:
+        pl.semaphore_signal(barrier, inc=1, device_id=dp_source(step), device_id_type=MESH)
+        greeted += 1
+    for step in range(1, n_seq):
+        pl.semaphore_signal(
+            barrier, inc=1, device_id={"seq": seq_peer(step)}, device_id_type=MESH
+        )
+        greeted += 1
+    for step in range(1, n_head):
+        pl.semaphore_signal(
+            barrier, inc=1, device_id={"head": head_peer(step)}, device_id_type=MESH
+        )
+        greeted += 1
+    pl.semaphore_wait(barrier, greeted)
+
+    def dp_copy(c, step):
+        return remote(
+            dq_ref.at[c], gath.at[c, step - 1],
+            d_ss.at[c, step - 1], d_rs.at[c, step - 1], dp_peer(step),
+        )
+
+    def relay_copy(c, via, onward):
+        return remote(
+            gath.at[c, via - 1], gath.at[c, 2], d_ss.at[c, 2], d_rs.at[c, 2], dp_peer(onward)
+        )
+
+    @pl.loop(0, chunks)
+    def _(c):
+        for step in direct:
+            dp_copy(c, step).start()
+
+    gx_acc[...] = jnp.zeros_like(gx_acc)
+
+    def z_copy(c, step):
+        return remote(
+            z_send.at[c, seq_peer(step)], z_recv.at[c, step - 1],
+            z_ss.at[c, step - 1], z_rs.at[c, step - 1], {"seq": seq_peer(step)},
+        )
+
+    def input_share(c):
+        w_copy(c).wait()
+        gx_acc[...] += lax.dot_general(
+            dq_ref[c], w_buf[c], (((1,), (1,)), ((), ())), preferred_element_type=jnp.float32
+        )
+
+    def weight_share(c):
+        if relay:
+            relay_copy(c, 1, 2).wait_recv()
+        others = gath[c].reshape((n_dp - 1) * slab, width)
+        product = jnp.dot(lat_ref[:, :slab], dq_ref[c], preferred_element_type=jnp.float32)
+        product += jnp.dot(lat_ref[:, slab:], others, preferred_element_type=jnp.float32)
+        product = product.reshape(n_seq, rows, width)
+        part[...] = product
+        z_send[c] = product.astype(jnp.bfloat16)
+        for step in range(n_seq - 1, 0, -1):
+            z_copy(c, step).start()
+        gw_ref[c] = part[me_seq]
+
+    @pl.loop(0, chunks)
+    def _(c):
+        for step in direct:
+            dp_copy(c, step).wait_recv()
+        if relay:
+            @pl.when(lax.rem(c, 2) == 0)
+            def _():
+                relay_copy(c, 1, 2).start()
+
+            @pl.when(lax.rem(c, 2) == 1)
+            def _():
+                relay_copy(c, 2, 1).start()
+
+        input_share(c)
+
+        @pl.when(c > 0)
+        def _():
+            weight_share(c - 1)
+
+    def h_copy(step):
+        return remote(
+            gx_acc.at[pl.ds(pl.multiple_of(head_peer(step) * half, half), half)],
+            gx_recv.at[step - 1], h_ss.at[step - 1], h_rs.at[step - 1],
+            {"head": head_peer(step)},
+        )
+
+    for step in range(1, n_head):
+        h_copy(step).start()
+    weight_share(chunks - 1)
+    for step in range(1, n_head):
+        h_copy(step).wait()
+    total = gx_acc[pl.ds(pl.multiple_of(me_head * half, half), half)]
+    for step in range(1, n_head):
+        total = total + gx_recv[step - 1]
+    gx_ref[...] = total.astype(gx_ref.dtype)
+
+    @pl.loop(0, chunks)
+    def _(c):
+        for step in range(1, n_seq):
+            z_copy(c, step).wait()
+        share = gw_ref[c]
+        for step in range(1, n_seq):
+            share = share + z_recv[c, step - 1].astype(jnp.float32)
+        gw_ref[c] = share
+        for step in direct:
+            dp_copy(c, step).wait_send()
+        if relay:
+            relay_copy(c, 1, 2).wait_send()
+
+
+def grads(d_chunks, lat_t, flat_w):
+    n_dp, n_seq, n_head = (lax.axis_size(axis) for axis in ("dp", "seq", "head"))
+    chunks, slab, width = d_chunks.shape
+    model_width = flat_w.shape[0]
+    rows = model_width // (n_dp * n_seq)
+    half = slab // n_head
+    vmem = pl.BlockSpec(memory_space=pltpu.VMEM)
+    dma = pltpu.SemaphoreType.DMA
+    return pl.pallas_call(
+        functools.partial(grads_kernel, n_dp, n_seq, n_head),
+        out_shape=(
+            jax.ShapeDtypeStruct((chunks, rows, width), jnp.float32),
+            jax.ShapeDtypeStruct((half, model_width), jnp.bfloat16),
+        ),
+        in_specs=[vmem, vmem, pl.BlockSpec(memory_space=pl.ANY)],
+        out_specs=(vmem, vmem),
+        scratch_shapes=[
+            pltpu.VMEM((chunks, n_dp - 1, slab, width), jnp.bfloat16),
+            pltpu.VMEM((chunks, model_width, width), jnp.bfloat16),
+            pltpu.VMEM((n_seq, rows, width), jnp.float32),
+            pltpu.VMEM((chunks, n_seq, rows, width), jnp.bfloat16),
+            pltpu.VMEM((chunks, n_seq - 1, rows, width), jnp.bfloat16),
+            pltpu.VMEM((slab, model_width), jnp.float32),
+            pltpu.VMEM((n_head - 1, half, model_width), jnp.float32),
+            dma((chunks,)),
+            dma((chunks, n_dp - 1)),
+            dma((chunks, n_dp - 1)),
+            dma((chunks, n_seq - 1)),
+            dma((chunks, n_seq - 1)),
+            dma((n_head - 1,)),
+            dma((n_head - 1,)),
+        ],
+        compiler_params=pltpu.CompilerParams(
+            collective_id=0, has_side_effects=True, vmem_limit_bytes=60 * 1024 * 1024
+        ),
+        name="grads",
+    )(d_chunks, lat_t, flat_w)
+
+
+def clip_columns(slab_tokens):
+    n_dp = lax.axis_size("dp")
+    me = lax.axis_index("dp")
+    width = slab_tokens.shape[1] // n_dp
+    pieces = []
+    for step in range(n_dp):
+        if n_dp == 4:
+            pairs = [(i, i ^ step) for i in range(n_dp)]
+            target = me ^ step
+        else:
+            pairs = [(i, (i + step) % n_dp) for i in range(n_dp)]
+            target = lax.rem(me + step, n_dp)
+        piece = lax.dynamic_slice_in_dim(slab_tokens, target * width, width, 1)
+        pieces.append(lax.ppermute(piece, "dp", pairs) if step else piece)
+    return jnp.transpose(jnp.concatenate(pieces, axis=0))
 
 
 def local(latents, w_qkv, q_gain, k_gain, neighbours, grad_out):
@@ -129,29 +358,12 @@
         .astype(jnp.bfloat16)
         .reshape(slab_rows, 3 * head_width)
     )
-    grad_rows = lax.psum_scatter(
-        lax.dot_general(
-            d_qkv, flat_w, (((1,), (1,)), ((), ())), preferred_element_type=jnp.float32
-        ),
-        "head",
-        scatter_dimension=0,
-        tiled=True,
-    )
-    grad_x = grad_rows.astype(jnp.bfloat16)[None]
-    product = lax.dot_general(
-        slab_tokens, d_qkv, (((0,), (0,)), ((), ())), preferred_element_type=jnp.float32
-    )
-    clip_share = lax.psum_scatter(
-        product.reshape(
-            model_width // lax.axis_size("dp") * lax.axis_size("dp"), 3, head_width
-        ).astype(jnp.bfloat16),
-        "dp",
-        scatter_dimension=0,
-        tiled=True,
-    )
-    grad_w = lax.psum_scatter(clip_share, "seq", scatter_dimension=0, tiled=True).astype(
-        jnp.float32
-    )
+    width = 3 * HD
+    chunks = 3 * head_width // width
+    d_chunks = jnp.transpose(d_qkv.reshape(slab_rows, chunks, width), (1, 0, 2))
+    share, grad_rows = grads(d_chunks, clip_columns(slab_tokens), flat_w)
+    grad_x = grad_rows[None]
+    grad_w = jnp.transpose(share, (1, 0, 2)).reshape(share.shape[1], 3, head_width)
     return (attn_out, grad_x, grad_w)
 
 

time: 277 us -> 213 us (0.77)
  waiting for transfers between devices: 145 us -> 0.02 us
  Pallas kernels: 0 us -> 88.4 us
  local copies, waits for them, and re-layouts: 40.6 us -> 59.5 us
  matrix products: 41.8 us -> 27.9 us
  between operations: 14.2 us -> 1.07 us
  starting transfers between devices: 20.8 us -> 23.7 us
    reduce_scatter x3 -> x0, waiting for transfers between devices: 145 us -> none  [the longest x1 89.1 us: local(): lax.psum_scatter(product.reshape(model_width // lax.axis_size('dp') * lax...]
    pallas_call x0 -> x1, Pallas kernels: none -> 88.4 us  [grads(): pl.pallas_call(functools.partial(grads_kernel, n_dp, n_seq, n_head), out_...]
    dot_general x2 -> x0, matrix products: 12.8 us -> none  [the longest x1 7.72 us: local(): lax.dot_general(d_qkv, flat_w, (((1,), (1,)), ((), ())), preferred_elemen...]
    reshape x0 -> x1, local copies, waits for them, and re-layouts: none -> 12.6 us  [local(): flat_w = w_qkv.reshape(model_width, 3 * head_width)]
    convert_element_type x1, local copies, waits for them, and re-layouts: 12.6 us -> 1.41 us  [local(): d_qkv = jnp.stack([d_query, d_key, d_value], axis=1).astype(jnp.bfloat16)...]
    dynamic_slice x0 -> x5, local copies, waits for them, and re-layouts: none -> 8.34 us  [clip_columns(): piece = lax.dynamic_slice_in_dim(slab_tokens, target * width, width, 1)]
    ppermute x0 -> x3, starting transfers between devices: none -> 3.49 us  [clip_columns(): pieces.append(lax.ppermute(piece, 'dp', pairs) if step else piece)]
    unnamed x43 -> x45, local copies, waits for them, and re-layouts: 19.4 us -> 22 us
  transfers between devices with their start and end apart: 9 -> 9, of which waited for: 3 -> 0; matrix products, arithmetic and copies ran while one was open for 13% -> 24% of each run, Pallas kernels for 0% -> 0%
where the time goes in v1:
time: 213 us; the launch traced here: 212 us
  Pallas kernels  88.4 us (42%)
  local copies, waits for them, and re-layouts  59.5 us (28%)
  matrix products  27.9 us (13%)
  starting transfers between devices  23.7 us (11%)
  other arithmetic  11.3 us (5%)
    pallas_call x1, Pallas kernels, grads(): pl.pallas_call(functools.partial(grads_kernel, n_dp, n_seq, n_head), out_...  88.4 us
    unnamed x45, local copies, waits for them, and re-layouts  22 us
    ppermute x3, starting transfers between devices, with_halo(): lax.ppermute(lax.slice_in_dim(block, block.shape[dim] - width, None, axis...  16.2 us
    reshape x1, local copies, waits for them, and re-layouts, local(): flat_w = w_qkv.reshape(model_width, 3 * head_width)  12.6 us
    dynamic_slice x5, local copies, waits for them, and re-layouts, clip_columns(): piece = lax.dynamic_slice_in_dim(slab_tokens, target * width, width, 1)  8.34 us
    dot_general x1, matrix products, local(): jnp.einsum('hqk,khe->qhe', d_scores, keys_wide, preferred_element_type=jn...  6.36 us
    dot_general x1, matrix products, local(): jnp.dot(slab_tokens, flat_w, preferred_element_type=jnp.float32)  5.24 us
    dot_general x1, matrix products, local(): jnp.einsum('hqk,qhe->khe', d_scores_back, queries_wide, preferred_element...  4.93 us
  transfers between devices with their start and end apart: 9, of which 0 were waited for; matrix products, arithmetic and copies ran while one was open for 24% of the time, Pallas kernels for 0%

profile of v1, /device:TPU:0, one launch (start us, length us, event | category | flops | bytes accessed | tf_op | source)
XLA Modules:
  0.0 212.0 jit_solution(8418518750102486265)
XLA Ops:
  0.6 12.8 %copy.93 = bf16[2048,3,768]{0,2,1:T(8,128)(2,1)} copy(bf16[2048,3,768]{2,0,1:T(8,128)(2,1)} %param.7) | data formatting | bytes 18874368 | tf_op args[1]
  13.5 5.2 %fusion.36 = f32[256,3,6,128]{0,3,2,1:T(8,128)S(1)} fusion(bf16[3,6,128,2048]{3,2,1,0:T(8,128)(2,1)} %bitcast.149, bf16[1,256,2048]{2,1,0:T(8,128)(2,1)S(1)} %copy-done.7), kind=kOutput, calls=%fused_computation.33 | convolution fusion | flops 2415919104 | bytes 12845056 | tf_op jit(solution)/shard_map/dot_general | solution.py:290
  18.8 1.0 fusion.60
  19.8 0.1 fusion.40
  20.0 0.2 fusion.42
  20.2 1.0 pad_maximum_fusion.3
  21.2 1.3 collective-permute-start.1
  22.5 6.5 %collective-permute-start = (bf16[256,2,768]{0,2,1:T(8,128)(2,1)}, bf16[256,2,768]{0,2,1:T(8,128)(2,1)}, u32[]{:S(2)}, u32[]{:S(2)}) collective-permute-start(bf16[256,2,768]{0,2,1:T(8,128)(2,1)} %pad_maximum_fusion.3), channel_id=1, source_target_pairs={{0,2},{2,4},{4,6},{1,3},{3,5},{5,7},{8,10},{10,12},{12,14},{9,11},... | collective-permute-start | bytes 2359304 | tf_op jit(solution)/shard_map/ppermute | solution.py:25
  29.0 2.1 constant_dynamic-slice_fusion.3
  31.1 1.8 copy.114
  32.9 2.9 %collective-permute-start.8 = (bf16[256,512]{0,1:T(8,128)(2,1)}, bf16[256,512]{0,1:T(8,128)(2,1)}, u32[]{:S(2)}, u32[]{:S(2)}) collective-permute-start(bf16[256,512]{0,1:T(8,128)(2,1)} %bitcast.177), channel_id=1, source_target_pairs={{0,24},{8,16},{16,8},{24,0},{1,25},{9,17},{17,9},{25,1},{2,26},{10... | collective-permute-start | bytes 786440 | tf_op jit(solution)/shard_map/ppermute | solution.py:277
  35.8 1.8 copy.113
  37.5 0.5 collective-permute-start.7
  38.0 0.9 copy.112
  38.9 0.1 collective-permute-start.6
  39.1 0.1 copy.96
  39.2 0.6 broadcast_bitcast_fusion
  39.8 0.1 copy.106
  39.9 0.1 compare_reduce_fusion.1
  40.0 0.1 and_select_fusion.1
  40.1 0.7 compare_reduce_fusion
  40.7 0.1 copy.97
  40.9 0.1 reshape.206
  41.0 1.0 broadcast_in_dim.33
  42.0 2.3 %copy.98 = f32[256,768]{1,0:T(8,128)} copy(f32[256,768]{0,1:T(8,128)} %bitcast.165) | data formatting | bytes 1572864 | tf_op jit(solution)/shard_map/mul | solution.py:315
  44.3 1.2 copy.99
  45.5 2.1 fusion.39
  47.7 0.7 broadcast_in_dim.61
  48.4 1.4 reshape.208
  49.8 1.6 broadcast_in_dim.62
  51.4 2.3 %copy.107 = f32[768,256]{1,0:T(8,128)} copy(f32[768,256]{0,1:T(8,128)} %bitcast.166) | data formatting | bytes 1572864 | tf_op jit(solution)/shard_map/mul | solution.py:340
  53.7 1.8 copy.111
  55.5 12.6 %copy.115.w_ref = bf16[2048,2304]{1,0:T(8,128)(2,1)} copy(bf16[2048,2304]{0,1:T(8,128)(2,1)} %bitcast.150) | data formatting | bytes 18874368 | tf_op jit(solution)/shard_map/reshape | solution.py:289
  68.2 1.1 pad_maximum_fusion.4
  69.2 1.3 collective-permute-start.3
  70.5 4.6 %collective-permute-start.2 = (bf16[256,2,768]{0,2,1:T(8,128)(2,1)S(1)}, bf16[256,2,768]{0,2,1:T(8,128)(2,1)S(1)}, u32[]{:S(2)}, u32[]{:S(2)}) collective-permute-start(bf16[256,2,768]{0,2,1:T(8,128)(2,1)S(1)} %pad_maximum_fusion.4), channel_id=1, source_target_pairs={{0,2},{2,4},{4,6},{1,3},{3,5},{5,7},{8,10},{10,12},{12,14},{9,11},... | collective-permute-start | bytes 2359304 | tf_op jit(solution)/shard_map/ppermute | solution.py:25
  75.2 2.4 %maximum_bitcast_fusion.lat_ref = bf16[512,1024]{1,0:T(8,128)(2,1)} fusion(bf16[256,512]{0,1:T(8,128)(2,1)} %collective-permute-done.8, bf16[256,512]{0,1:T(8,128)(2,1)} %collective-permute-done.7, bf16[256,512]{0,1:T(8,128)(2,1)} %collective-permute-done.6, bf16[256,512]{0,1:T(8,128)(2,1)} %bitcast.172), kind=kLoop, calls=%fused_computation.32 | loop fusion | flops 4194304 | bytes 2097152 | tf_op jit(solution)/shard_map/transpose | solution.py:278
  77.5 1.5 pad_maximum_fusion
  79.1 0.2 fusion.61
  79.3 1.0 copy-done.5
  80.3 1.4 fusion.5
  81.7 3.7 %fusion = (f32[6,256]{1,0:T(8,128)S(1)}, f32[6,768,256]{1,2,0:T(8,128)}) fusion(f32[6,256]{1,0:T(8,128)S(1)} %get-tuple-element.38, f32[256,768]{1,0:T(8,128)S(1)} %copy-done.5, f32[6,256,768]{2,1,0:T(8,128)S(1)} %get-tuple-element.39, bf16[768,6,128]{0,2,1:T(8,128)(2,1)S(1)} %bitcast.170, bf16[256,6,128]{0,2,1:T(8,128)(2,1)S(1)} %bitcast.163), kind=kOutput, calls=%fused_computation.2 | convolution fusion | flops 307886592 | bytes 11808768 | tf_op jit(solution)/shard_map/qhe,khe->hqk/dot_general | solution.py:322
  85.4 0.6 maximum_bitcast_fusion.1
  86.0 1.4 collective-permute-start.5
  87.4 5.2 %collective-permute-start.4 = (f32[256,2,6]{0,2,1:T(8,128)}, f32[256,2,6]{0,2,1:T(8,128)}, u32[]{:S(2)}, u32[]{:S(2)}) collective-permute-start(f32[256,2,6]{0,2,1:T(8,128)} %maximum_bitcast_fusion.1), channel_id=1, source_target_pairs={{0,2},{2,4},{4,6},{1,3},{3,5},{5,7},{8,10},{10,12},{12,14},{9,11},... | collective-permute-start | bytes 36872 | tf_op jit(solution)/shard_map/ppermute | solution.py:25
  92.6 2.0 fusion.27
  94.6 0.2 pad_maximum_fusion.1
  94.8 1.2 fusion.59
  95.9 1.9 copy.117
  97.8 0.8 pad_maximum_fusion.5
  98.6 0.6 slice_bitcast_fusion
  99.2 3.1 %multiply_divide_fusion = f32[6,768,256]{2,1,0:T(8,128)S(1)} fusion(f32[6,768]{1,0:T(8,128)S(1)} %compare_select_fusion, f32[768,256]{1,0:T(8,128)} %copy.107, bf16[768,6,128]{0,2,1:T(8,128)(2,1)} %bitcast.153, f32[128]{0:T(128)} %param.9, f32[256,6]{0,1:T(8,128)S(1)} %get-tuple-element.44, f32[256,3,6,128]{0,3,2,1:T(8,128)S(1)} %fusion.36), kind=kOutput, calls=%fused_computation.7 | convolution fusion | flops 306118656 | bytes 7504384 | tf_op jit(solution)/shard_map/qhe,khe->hqk/dot_general | solution.py:337
  102.3 2.2 %copy-done = f32[6,768,256]{2,1,0:T(8,128)} copy-done((f32[6,768,256]{2,1,0:T(8,128)}, f32[6,768,256]{2,1,0:T(8,128)S(1)}, u32[]{:S(2)}) %copy-start) | copy-done | bytes 4718616
  104.5 1.3 fusion.33
  105.8 4.9 %fusion.26 = f32[256,6,128]{0,2,1:T(8,128)} fusion(bf16[768,6,128]{0,2,1:T(8,128)(2,1)} %bitcast.154, f32[6,768,256]{2,1,0:T(8,128)} %copy-done, bf16[768,6,128]{0,2,1:T(8,128)(2,1)S(1)} %bitcast.152, f32[6,768]{1,0:T(8,128)} %slice_bitcast_fusion, f32[128]{0:T(128)} %param.9, f32[256,3,6,128]{0,3,2,1:T(8,128)S(1)} %fusion.36), kind=kOutput, calls=%fused_computation.27 | convolution fusion | flops 608894976 | bytes 8276480 | tf_op jit(solution)/shard_map/hqk,qhe->khe/dot_general | solution.py:348
  110.7 6.4 %multiply_reduce_fusion.1 = (f32[256,6]{0,1:T(8,128)S(1)}, f32[256,6]{0,1:T(8,128)S(1)}, f32[256,6,128]{0,2,1:T(8,128)S(1)}) fusion(f32[256,6]{0,1:T(8,128)S(1)} %get-tuple-element.43, f32[256,3,6,128]{0,3,2,1:T(8,128)S(1)} %fusion.36, f32[256,6,128]{0,2,1:T(8,128)} %fusion.26, f32[256,6]{0,1:T(8,128)S(1)} %get-tuple-element.44, f32[128]{0:T(128)} %param.8, ...), kind=kOutput, calls=%fused_computation.54 | convolution fusion | flops 311620608 | bytes 14586368 | tf_op jit(solution)/shard_map/hqk,khe->qhe/dot_general | solution.py:325
  117.2 0.4 fusion.45
  117.5 0.6 copy-done.6
  118.1 0.1 pad_maximum_fusion.2
  118.2 1.4 copy.110
  119.7 88.4 %grads.1 = (f32[6,128,384]{2,1,0:T(8,128)}, bf16[128,2048]{1,0:T(8,128)(2,1)}) custom-call(bf16[6,256,384]{2,1,0:T(8,128)(2,1)} %bitcast.157, bf16[512,1024]{1,0:T(8,128)(2,1)} %maximum_bitcast_fusion.lat_ref, bf16[2048,2304]{1,0:T(8,128)(2,1)} %copy.115.w_ref), custom_call_target="tpu_custom_call" | custom-call | tf_op jit(solution)/shard_map/grads/pallas_call | solution.py:233
  208.1 1.7 copy.116
  209.8 1.4 copy.118
  211.2 0.8 copy.130
  (62 shorter events, 0.5 us)
Async XLA Ops:
  0.6 12.8 %copy-start.7 = (bf16[1,256,2048]{2,1,0:T(8,128)(2,1)S(1)}, bf16[1,256,2048]{2,1,0:T(8,128)(2,1)}, u32[]{:S(2)}) copy-start(bf16[1,256,2048]{2,1,0:T(8,128)(2,1)} %param.6) | copy-start | bytes 3145732
  18.7 1.2 copy-start.12
  20.2 18.9 %copy-start.9 = (s32[16,9]{1,0:T(8,128)S(1)}, s32[16,9]{1,0:T(8,128)}, u32[]{:S(2)}) copy-start(s32[16,9]{1,0:T(8,128)} %param.10) | copy-start | bytes 1732
  20.2 19.0 %copy-start.18 = (f32[128]{0:T(128)S(1)}, f32[128]{0:T(128)}, u32[]{:S(2)}) copy-start(f32[128]{0:T(128)} %param.8) | copy-start | bytes 1540
  21.2 56.4 %collective-permute-start.1 = (bf16[256,2,768]{0,2,1:T(8,128)(2,1)}, bf16[256,2,768]{0,2,1:T(8,128)(2,1)}, u32[]{:S(2)}, u32[]{:S(2)}) collective-permute-start(bf16[256,2,768]{0,2,1:T(8,128)(2,1)} %pad_maximum_fusion.3), channel_id=1, source_target_pairs={{2,0},{4,2},{6,4},{3,1},{5,3},{7,5},{10,8},{12,10},{14,12},{11,9},... | collective-permute-start | bytes 2359304 | tf_op jit(solution)/shard_map/ppermute | solution.py:28
  22.5 55.1 %collective-permute-start = (bf16[256,2,768]{0,2,1:T(8,128)(2,1)}, bf16[256,2,768]{0,2,1:T(8,128)(2,1)}, u32[]{:S(2)}, u32[]{:S(2)}) collective-permute-start(bf16[256,2,768]{0,2,1:T(8,128)(2,1)} %pad_maximum_fusion.3), channel_id=1, source_target_pairs={{0,2},{2,4},{4,6},{1,3},{3,5},{5,7},{8,10},{10,12},{12,14},{9,11},... | collective-permute-start | bytes 2359304 | tf_op jit(solution)/shard_map/ppermute | solution.py:25
  32.9 36.4 %collective-permute-start.8 = (bf16[256,512]{0,1:T(8,128)(2,1)}, bf16[256,512]{0,1:T(8,128)(2,1)}, u32[]{:S(2)}, u32[]{:S(2)}) collective-permute-start(bf16[256,512]{0,1:T(8,128)(2,1)} %bitcast.177), channel_id=1, source_target_pairs={{0,24},{8,16},{16,8},{24,0},{1,25},{9,17},{17,9},{25,1},{2,26},{10... | collective-permute-start | bytes 786440 | tf_op jit(solution)/shard_map/ppermute | solution.py:277
  37.5 33.0 %collective-permute-start.7 = (bf16[256,512]{0,1:T(8,128)(2,1)}, bf16[256,512]{0,1:T(8,128)(2,1)}, u32[]{:S(2)}, u32[]{:S(2)}) collective-permute-start(bf16[256,512]{0,1:T(8,128)(2,1)} %bitcast.176), channel_id=1, source_target_pairs={{0,16},{8,24},{16,0},{24,8},{1,17},{9,25},{17,1},{25,9},{2,18},{10... | collective-permute-start | bytes 786440 | tf_op jit(solution)/shard_map/ppermute | solution.py:277
  38.9 36.2 %collective-permute-start.6 = (bf16[256,512]{0,1:T(8,128)(2,1)}, bf16[256,512]{0,1:T(8,128)(2,1)}, u32[]{:S(2)}, u32[]{:S(2)}) collective-permute-start(bf16[256,512]{0,1:T(8,128)(2,1)} %bitcast.175), channel_id=1, source_target_pairs={{0,8},{8,0},{16,24},{24,16},{1,9},{9,1},{17,25},{25,17},{2,10},{10... | collective-permute-start | bytes 786440 | tf_op jit(solution)/shard_map/ppermute | solution.py:277
  39.0 3.0 %copy-start.13 = (pred[12]{0:T(512)(128)(4,1)}, pred[12]{0:T(512)(128)(4,1)S(1)}, u32[]{:S(2)}) copy-start(pred[12]{0:T(512)(128)(4,1)S(1)} %compare_and_fusion) | copy-start | bytes 40
  39.0 2.9 %copy-start.15 = (pred[4]{0:T(512)(128)(4,1)}, pred[4]{0:T(512)(128)(4,1)S(1)}, u32[]{:S(2)}) copy-start(pred[4]{0:T(512)(128)(4,1)S(1)} %compare_and_fusion.1) | copy-start | bytes 16
  45.4 2.2 %copy-start.14 = (pred[12]{0:T(512)(128)(4,1)S(1)}, pred[12]{0:T(512)(128)(4,1)}, u32[]{:S(2)}) copy-start(pred[12]{0:T(512)(128)(4,1)} %copy-done.13) | copy-start | bytes 40
  45.4 2.1 %copy-start.16 = (pred[4]{0:T(512)(128)(4,1)S(1)}, pred[4]{0:T(512)(128)(4,1)}, u32[]{:S(2)}) copy-start(pred[4]{0:T(512)(128)(4,1)} %copy-done.15) | copy-start | bytes 16
  45.4 2.1 %copy-start.17 = (pred[12,4]{0,1:T(4,128)(4,1)S(1)}, pred[12,4]{0,1:T(4,128)(4,1)}, u32[]{:S(2)}) copy-start(pred[12,4]{0,1:T(4,128)(4,1)} %compare_reduce_fusion) | copy-start | bytes 148
  69.2 25.3 %collective-permute-start.3 = (bf16[256,2,768]{0,2,1:T(8,128)(2,1)S(1)}, bf16[256,2,768]{0,2,1:T(8,128)(2,1)S(1)}, u32[]{:S(2)}, u32[]{:S(2)}) collective-permute-start(bf16[256,2,768]{0,2,1:T(8,128)(2,1)S(1)} %pad_maximum_fusion.4), channel_id=1, source_target_pairs={{2,0},{4,2},{6,4},{3,1},{5,3},{7,5},{10,8},{12,10},{14,12},{11,9},... | collective-permute-start | bytes 2359304 | tf_op jit(solution)/shard_map/ppermute | solution.py:28
  70.5 24.0 %collective-permute-start.2 = (bf16[256,2,768]{0,2,1:T(8,128)(2,1)S(1)}, bf16[256,2,768]{0,2,1:T(8,128)(2,1)S(1)}, u32[]{:S(2)}, u32[]{:S(2)}) collective-permute-start(bf16[256,2,768]{0,2,1:T(8,128)(2,1)S(1)} %pad_maximum_fusion.4), channel_id=1, source_target_pairs={{0,2},{2,4},{4,6},{1,3},{3,5},{5,7},{8,10},{10,12},{12,14},{9,11},... | collective-permute-start | bytes 2359304 | tf_op jit(solution)/shard_map/ppermute | solution.py:25
  79.1 1.2 copy-start.5
  79.1 1.2 copy-start.19
  79.3 2.4 %copy-start.2 = (bf16[768,1,768]{0,2,1:T(8,128)(2,1)}, bf16[768,1,768]{0,2,1:T(8,128)(2,1)S(1)}, u32[]{:S(2)}) copy-start(bf16[768,1,768]{0,2,1:T(8,128)(2,1)S(1)} %get-tuple-element.32) | copy-start | bytes 3538948
  81.7 10.9 %copy-start.1 = (f32[6,256,768]{2,1,0:T(8,128)}, f32[6,256,768]{2,1,0:T(8,128)S(1)}, u32[]{:S(2)}) copy-start(f32[6,256,768]{2,1,0:T(8,128)S(1)} %get-tuple-element.39) | copy-start | bytes 14155780
  81.7 10.9 %copy-start.10 = (f32[6,256]{1,0:T(8,128)}, f32[6,256]{1,0:T(8,128)S(1)}, u32[]{:S(2)}) copy-start(f32[6,256]{1,0:T(8,128)S(1)} %get-tuple-element.38) | copy-start | bytes 18436
  85.4 9.2 %copy-start.11 = (f32[6,256]{1,0:T(8,128)}, f32[6,256]{1,0:T(8,128)S(1)}, u32[]{:S(2)}) copy-start(f32[6,256]{1,0:T(8,128)S(1)} %get-tuple-element.40) | copy-start | bytes 18436
  86.0 8.6 %copy-start.3 = (bf16[256,1,768]{0,2,1:T(8,128)(2,1)S(1)}, bf16[256,1,768]{0,2,1:T(8,128)(2,1)}, u32[]{:S(2)}) copy-start(bf16[256,1,768]{0,2,1:T(8,128)(2,1)} %fusion.39) | copy-start | bytes 1179652
  86.0 11.8 %collective-permute-start.5 = (f32[256,2,6]{0,2,1:T(8,128)}, f32[256,2,6]{0,2,1:T(8,128)}, u32[]{:S(2)}, u32[]{:S(2)}) collective-permute-start(f32[256,2,6]{0,2,1:T(8,128)} %maximum_bitcast_fusion.1), channel_id=1, source_target_pairs={{2,0},{4,2},{6,4},{3,1},{5,3},{7,5},{10,8},{12,10},{14,12},{11,9},... | collective-permute-start | bytes 36872 | tf_op jit(solution)/shard_map/ppermute | solution.py:28
  87.4 10.4 %collective-permute-start.4 = (f32[256,2,6]{0,2,1:T(8,128)}, f32[256,2,6]{0,2,1:T(8,128)}, u32[]{:S(2)}, u32[]{:S(2)}) collective-permute-start(f32[256,2,6]{0,2,1:T(8,128)} %maximum_bitcast_fusion.1), channel_id=1, source_target_pairs={{0,2},{2,4},{4,6},{1,3},{3,5},{5,7},{8,10},{10,12},{12,14},{9,11},... | collective-permute-start | bytes 36872 | tf_op jit(solution)/shard_map/ppermute | solution.py:25
  102.3 2.2 %copy-start = (f32[6,768,256]{2,1,0:T(8,128)}, f32[6,768,256]{2,1,0:T(8,128)S(1)}, u32[]{:S(2)}) copy-start(f32[6,768,256]{2,1,0:T(8,128)S(1)} %multiply_divide_fusion) | copy-start | bytes 14155780
  110.7 6.4 %copy-start.4 = (f32[256,6,128]{0,2,1:T(8,128)S(1)}, f32[256,6,128]{0,2,1:T(8,128)}, u32[]{:S(2)}) copy-start(f32[256,6,128]{0,2,1:T(8,128)} %fusion.26) | copy-start | bytes 2359300
  117.1 1.0 copy-start.6
  208.1 3.1 %copy-start.8 = (bf16[128,2048]{1,0:T(8,128)(2,1)S(1)}, bf16[128,2048]{1,0:T(8,128)(2,1)}, u32[]{:S(2)}) copy-start(bf16[128,2048]{1,0:T(8,128)(2,1)} %get-tuple-element.5) | copy-start | bytes 1572868

commit v2 on v1

v2 whole, which is shorter than its diff:
```python
import functools
import math

import jax
import jax.numpy as jnp
from jax import lax
from jax.experimental import pallas as pl
from jax.experimental.pallas import tpu as pltpu
from jax.sharding import PartitionSpec as P

MESH = pl.DeviceIdType.MESH

HD = 128
TILE = 64


EPS = 1e-06


def inv_rms(values):
    return lax.rsqrt(jnp.mean(values * values, axis=-1, keepdims=True) + EPS)


def norm_back(raw, inverse, gain, upstream):
    normed = raw * inverse
    weighted = upstream * gain
    return inverse * (weighted - normed * jnp.mean(weighted * normed, axis=-1, keepdims=True))


def remote(src, dst, send_sem, recv_sem, peer):
    return pltpu.make_async_remote_copy(
        src_ref=src,
        dst_ref=dst,
        send_sem=send_sem,
        recv_sem=recv_sem,
        device_id=peer,
        device_id_type=MESH,
    )


def grads_kernel(
    n_dp, n_seq, n_head, dq_ref, lat_ref, w_ref, gw_ref, gx_ref,
    gath, w_buf, part, z_send, z_recv, gx_acc, gx_recv,
    w_sem, d_ss, d_rs, z_ss, z_rs, h_ss, h_rs,
):
    chunks, slab, width = dq_ref.shape
    rows = part.shape[1]
    half = gx_ref.shape[0]
    me_dp = lax.axis_index("dp")
    me_seq = lax.axis_index("seq")
    me_head = lax.axis_index("head")
    relay = n_dp == 4
    parts = chunks // w_ref.shape[0]

    def cols(c):
        return pl.ds(pl.multiple_of(lax.rem(c, parts) * width, width), width)

    def dp_peer(step):
        if relay:
            low, high = lax.rem(me_dp, 2), me_dp // 2
            if step % 2:
                low = 1 - low
            if step // 2:
                high = 1 - high
            return {"dp": high * 2 + low}
        return {"dp": lax.rem(me_dp + step, n_dp)}

    def dp_source(step):
        if relay:
            return dp_peer(step)
        return {"dp": lax.rem(me_dp + n_dp - step, n_dp)}

    direct = (1, 2) if relay else tuple(range(1, n_dp))

    def seq_peer(step):
        return lax.rem(me_seq + step, n_seq)

    def head_peer(step):
        return lax.rem(me_head + step, n_head)

    def w_copy(c):
        return pltpu.make_async_copy(w_ref.at[c // parts, :, cols(c)], w_buf.at[c], w_sem.at[c])

    @pl.loop(0, chunks)
    def _(c):
        w_copy(c).start()

    barrier = pltpu.get_barrier_semaphore()
    greeted = 0
    for step in direct:
        pl.semaphore_signal(barrier, inc=1, device_id=dp_source(step), device_id_type=MESH)
        greeted += 1
    for step in range(1, n_seq):
        pl.semaphore_signal(
            barrier, inc=1, device_id={"seq": seq_peer(step)}, device_id_type=MESH
        )
        greeted += 1
    for step in range(1, n_head):
        pl.semaphore_signal(
            barrier, inc=1, device_id={"head": head_peer(step)}, device_id_type=MESH
        )
        greeted += 1
    pl.semaphore_wait(barrier, greeted)

    def dp_copy(c, step):
        return remote(
            dq_ref.at[c], gath.at[c, step - 1],
            d_ss.at[c, step - 1], d_rs.at[c, step - 1], dp_peer(step),
        )

    def relay_copy(c, via, onward):
        return remote(
            gath.at[c, via - 1], gath.at[c, 2], d_ss.at[c, 2], d_rs.at[c, 2], dp_peer(onward)
        )

    @pl.loop(0, chunks)
    def _(c):
        for step in direct:
            dp_copy(c, step).start()

    gx_acc[...] = jnp.zeros_like(gx_acc)

    def z_copy(c, step):
        return remote(
            z_send.at[c, seq_peer(step)], z_recv.at[c, step - 1],
            z_ss.at[c, step - 1], z_rs.at[c, step - 1], {"seq": seq_peer(step)},
        )

    def input_share(c):
        w_copy(c).wait()
        gx_acc[...] += lax.dot_general(
            dq_ref[c], w_buf[c], (((1,), (1,)), ((), ())), preferred_element_type=jnp.float32
        )

    def weight_share(c):
        if relay:
            relay_copy(c, 1, 2).wait_recv()
        others = gath[c].reshape((n_dp - 1) * slab, width)
        product = jnp.dot(lat_ref[:, :slab], dq_ref[c], preferred_element_type=jnp.float32)
        product += jnp.dot(lat_ref[:, slab:], others, preferred_element_type=jnp.float32)
        product = product.reshape(n_seq, rows, width)
        part[...] = product
        z_send[c] = product.astype(jnp.bfloat16)
        for step in range(n_seq - 1, 0, -1):
            z_copy(c, step).start()
        gw_ref[c // parts, :, cols(c)] = part[me_seq]

    @pl.loop(0, chunks)
    def _(c):
        for step in direct:
            dp_copy(c, step).wait_recv()
        if relay:
            @pl.when(lax.rem(c, 2) == 0)
            def _():
                relay_copy(c, 1, 2).start()

            @pl.when(lax.rem(c, 2) == 1)
            def _():
                relay_copy(c, 2, 1).start()

        input_share(c)

        @pl.when(c > 0)
        def _():
            weight_share(c - 1)

    def h_copy(step):
        return remote(
            gx_acc.at[pl.ds(pl.multiple_of(head_peer(step) * half, half), half)],
            gx_recv.at[step - 1], h_ss.at[step - 1], h_rs.at[step - 1],
            {"head": head_peer(step)},
        )

    for step in range(1, n_head):
        h_copy(step).start()
    weight_share(chunks - 1)
    for step in range(1, n_head):
        h_copy(step).wait()
    total = gx_acc[pl.ds(pl.multiple_of(me_head * half, half), half)]
    for step in range(1, n_head):
        total = total + gx_recv[step - 1]
    gx_ref[...] = total.astype(gx_ref.dtype)

    @pl.loop(0, chunks)
    def _(c):
        for step in range(1, n_seq):
            z_copy(c, step).wait()
        share = gw_ref[c // parts, :, cols(c)]
        for step in range(1, n_seq):
            share = share + z_recv[c, step - 1].astype(jnp.float32)
        gw_ref[c // parts, :, cols(c)] = share
        for step in direct:
            dp_copy(c, step).wait_send()
        if relay:
            relay_copy(c, 1, 2).wait_send()


def grads(d_chunks, lat_t, w_three):
    n_dp, n_seq, n_head = (lax.axis_size(axis) for axis in ("dp", "seq", "head"))
    chunks, slab, width = d_chunks.shape
    three, model_width, head_width = w_three.shape
    rows = model_width // (n_dp * n_seq)
    half = slab // n_head
    vmem = pl.BlockSpec(memory_space=pltpu.VMEM)
    dma = pltpu.SemaphoreType.DMA
    return pl.pallas_call(
        functools.partial(grads_kernel, n_dp, n_seq, n_head),
        out_shape=(
            jax.ShapeDtypeStruct((three, rows, head_width), jnp.float32),
            jax.ShapeDtypeStruct((half, model_width), jnp.bfloat16),
        ),
        in_specs=[vmem, vmem, pl.BlockSpec(memory_space=pl.ANY)],
        out_specs=(vmem, vmem),
        scratch_shapes=[
            pltpu.VMEM((chunks, n_dp - 1, slab, width), jnp.bfloat16),
            pltpu.VMEM((chunks, model_width, width), jnp.bfloat16),
            pltpu.VMEM((n_seq, rows, width), jnp.float32),
            pltpu.VMEM((chunks, n_seq, rows, width), jnp.bfloat16),
            pltpu.VMEM((chunks, n_seq - 1, rows, width), jnp.bfloat16),
            pltpu.VMEM((slab, model_width), jnp.float32),
            pltpu.VMEM((n_head - 1, half, model_width), jnp.float32),
            dma((chunks,)),
            dma((chunks, n_dp - 1)),
            dma((chunks, n_dp - 1)),
            dma((chunks, n_seq - 1)),
            dma((chunks, n_seq - 1)),
            dma((n_head - 1,)),
            dma((n_head - 1,)),
        ],
        compiler_params=pltpu.CompilerParams(
            collective_id=0, has_side_effects=True, vmem_limit_bytes=60 * 1024 * 1024
        ),
        name="grads",
    )(d_chunks, lat_t, w_three)


def layer_kernel(
    n_dp, n_seq, n_head, lat_ref, w_ref, qg_ref, kg_ref, near_ref, do_ref,
    out_ref, d_ref, latt_ref,
    lat_buf, w_buf, do_buf, q_raw, k_raw, q_hat, k_hat, v_hat, mask, mask_t, stat, stat_t, clip_buf,
    l_sem, w_sem, a_ss, a_rs, f_ss, f_rs, o_ss, o_rs, s_ss, s_rs, c_ss, c_rs,
):
    three, model_width, head_width = w_ref.shape
    slab = lat_ref.shape[0]
    chunks, _, width = d_ref.shape
    parts = chunks // three
    group = width // HD
    heads = head_width // HD
    half = slab // n_head
    block = model_width // n_dp
    scale = 1.0 / math.sqrt(HD)
    me_dp = lax.axis_index("dp")
    me_seq = lax.axis_index("seq")
    me_head = lax.axis_index("head")
    below = me_seq > 0
    above = me_seq < n_seq - 1

    def dp_peer(step, sign=1):
        if n_dp == 4:
            low, high = lax.rem(me_dp, 2), me_dp // 2
            if step % 2:
                low = 1 - low
            if step // 2:
                high = 1 - high
            return high * 2 + low
        return lax.rem(me_dp + n_dp + sign * step, n_dp)

    def head_peer(step, sign=1):
        return lax.rem(me_head + n_head + sign * step, n_head)

    own_lat = pltpu.make_async_copy(lat_ref, lat_buf.at[1], l_sem.at[0])
    own_do = pltpu.make_async_copy(do_ref, do_buf.at[1], l_sem.at[1])

    def cols(p):
        return pl.ds(pl.multiple_of(p * width, width), width)

    def w_copy(c):
        at = cols(lax.rem(c, parts))
        return pltpu.make_async_copy(
            w_ref.at[c // parts, :, at], w_buf.at[c // parts, :, at], w_sem.at[c]
        )

    own_lat.start()

    @pl.loop(0, chunks)
    def _(c):
        w_copy(c).start()

    own_do.start()

    barrier = pltpu.get_barrier_semaphore()

    @pl.when(below)
    def _():
        pl.semaphore_signal(barrier, inc=1, device_id={"seq": me_seq - 1}, device_id_type=MESH)

    @pl.when(above)
    def _():
        pl.semaphore_signal(barrier, inc=1, device_id={"seq": me_seq + 1}, device_id_type=MESH)

    for step in range(1, n_dp):
        pl.semaphore_signal(
            barrier, inc=1, device_id={"dp": dp_peer(step, -1)}, device_id_type=MESH
        )
    for step in range(1, n_head):
        pl.semaphore_signal(
            barrier, inc=1, device_id={"head": head_peer(step, -1)}, device_id_type=MESH
        )
    sides = jnp.minimum(me_seq, 1) + jnp.minimum(n_seq - 1 - me_seq, 1)
    pl.semaphore_wait(barrier, n_dp - 1 + n_head - 1 + sides)

    my_rows = pl.ds(pl.multiple_of(me_head * half, half), half)

    def lat_copy(side):
        return remote(
            lat_ref.at[my_rows], lat_buf.at[2 - 2 * side, my_rows],
            a_ss.at[side], a_rs.at[side], {"seq": me_seq + 2 * side - 1},
        )

    def do_copy(side):
        return remote(
            do_ref, do_buf.at[2 - 2 * side],
            o_ss.at[side], o_rs.at[side], {"seq": me_seq + 2 * side - 1},
        )

    def stat_copy(side):
        return remote(
            stat_t.at[1], stat_t.at[2 - 2 * side],
            s_ss.at[side], s_rs.at[side], {"seq": me_seq + 2 * side - 1},
        )

    def pass_copy(slot, step):
        return remote(
            lat_buf.at[slot, my_rows], lat_buf.at[slot, my_rows],
            f_ss.at[slot // 2, step - 1], f_rs.at[slot // 2, step - 1],
            {"head": head_peer(step)},
        )

    def clip_copy(step):
        peer = dp_peer(step)
        return remote(
            lat_ref.at[:, pl.ds(pl.multiple_of(peer * block, block), block)],
            clip_buf.at[step - 1], c_ss.at[step - 1], c_rs.at[step - 1], {"dp": peer},
        )

    @pl.when(below)
    def _():
        lat_copy(0).start()

    @pl.when(above)
    def _():
        lat_copy(1).start()

    for step in range(1, n_dp):
        clip_copy(step).start()

    @pl.when(below)
    def _():
        do_copy(0).start()

    @pl.when(above)
    def _():
        do_copy(1).start()

    def clear(slot):
        lat_buf[slot] = jnp.zeros_like(lat_buf[slot])
        do_buf[slot] = jnp.zeros_like(do_buf[slot])
        stat_t[slot] = jnp.ones_like(stat_t[slot])

    @pl.when(me_seq == 0)
    def _():
        clear(0)

    @pl.when(me_seq == n_seq - 1)
    def _():
        clear(2)

    tiles = near_ref.shape[0]
    near = near_ref[...]
    tile_ids = lax.broadcasted_iota(jnp.int32, (tiles, tiles), 1)
    hits = jnp.zeros((tiles, tiles), jnp.float32)
    for slot in range(near_ref.shape[1]):
        hits = jnp.where(near[:, slot : slot + 1] == tile_ids, 1.0, hits)
    hits = hits.astype(jnp.bfloat16)
    own_tile = me_seq * (slab // TILE)
    first_tile = own_tile - slab // TILE
    own_pick = lax.broadcasted_iota(jnp.int32, (slab, tiles), 1) == (
        lax.broadcasted_iota(jnp.int32, (slab, tiles), 0) // TILE + own_tile
    )
    own_pick = jnp.where(own_pick, 1.0, 0.0).astype(jnp.bfloat16)
    wide_pick = lax.broadcasted_iota(jnp.int32, (tiles, 3 * slab), 0) == (
        lax.broadcasted_iota(jnp.int32, (tiles, 3 * slab), 1) // TILE + first_tile
    )
    wide_pick = jnp.where(wide_pick, 1.0, 0.0).astype(jnp.bfloat16)
    picked = jnp.dot(own_pick, hits, preferred_element_type=jnp.float32).astype(jnp.bfloat16)
    mask[...] = jnp.dot(picked, wide_pick, preferred_element_type=jnp.float32)
    picked = lax.dot_general(
        own_pick, hits, (((1,), (1,)), ((), ())), preferred_element_type=jnp.float32
    ).astype(jnp.bfloat16)
    mask_t[...] = jnp.dot(picked, wide_pick, preferred_element_type=jnp.float32)

    q_gain = qg_ref[...]
    k_gain = kg_ref[...]
    own_lat.wait()

    def arrive(slot, side):
        lat_copy(side).wait_recv()
        for step in range(1, n_head):
            pass_copy(slot, step).start()

    def passed(slot):
        for step in range(1, n_head):
            pass_copy(slot, step).wait_recv()

    @pl.loop(0, 3)
    def _(turn):
        slot = lax.rem(turn + 1, 3)

        @pl.when(turn == 1)
        def _():
            @pl.when(above)
            def _():
                arrive(2, 0)

            @pl.when(below)
            def _():
                arrive(0, 1)

            @pl.when(above)
            def _():
                passed(2)

        @pl.when((turn == 2) & below)
        def _():
            passed(0)

        for kind in range(three):
            @pl.loop(0, parts)
            def _(p):
                @pl.when(turn == 0)
                def _():
                    w_copy(kind * parts + p).wait()

                raw = jnp.dot(
                    lat_buf[slot], w_buf[kind, :, cols(p)], preferred_element_type=jnp.float32
                )
                if kind == 2:
                    v_hat[slot, :, cols(p)] = raw.astype(jnp.bfloat16)
                else:
                    kept, normed, gain = ((q_raw, q_hat, q_gain), (k_raw, k_hat, k_gain))[kind]

                    @pl.when(turn == 0)
                    def _():
                        kept[:, cols(p)] = raw

                    pieces = []
                    for h in range(group):
                        piece = raw[:, h * HD : (h + 1) * HD]
                        pieces.append((piece * inv_rms(piece) * gain).astype(jnp.bfloat16))
                    normed[slot, :, cols(p)] = jnp.concatenate(pieces, axis=1)

    def at(h):
        return pl.ds(pl.multiple_of(h * HD, HD), HD)

    def nt(a, b):
        return lax.dot_general(a, b, (((1,), (1,)), ((), ())), preferred_element_type=jnp.float32)

    def put(kind, h, value):
        d_ref[kind * parts + h // group, :, at(lax.rem(h, group))] = value.astype(jnp.bfloat16)

    own_do.wait()
    lanes = lax.broadcasted_iota(jnp.int32, (slab, 128), 1)
    stat[...] = jnp.zeros_like(stat)

    @pl.loop(0, heads)
    def _(h):
        queries = q_hat[1, :, at(h)]
        keys = k_hat[:, :, at(h)].reshape(3 * slab, HD)
        values = v_hat[:, :, at(h)].reshape(3 * slab, HD)
        expo = jnp.exp(nt(queries, keys) * scale) * mask[...]
        row_total = jnp.sum(expo, axis=-1, keepdims=True)
        probs = expo * (1.0 / row_total)
        out_ref[:, at(h)] = jnp.dot(
            probs.astype(jnp.bfloat16), values, preferred_element_type=jnp.float32
        ).astype(jnp.bfloat16)
        d_probs = nt(do_buf[1, :, at(h)], values)
        row_delta = jnp.sum(probs * d_probs, axis=-1, keepdims=True)
        d_scores = (probs * (d_probs - row_delta) * scale).astype(jnp.bfloat16)
        d_qhat = jnp.dot(d_scores, keys, preferred_element_type=jnp.float32)
        raw = q_raw[:, at(h)]
        put(0, h, norm_back(raw, inv_rms(raw), q_gain, d_qhat))
        rows = jnp.where(lanes == 2 * h, row_total, stat[...])
        stat[...] = jnp.where(lanes == 2 * h + 1, row_delta, rows)

    stat_t[1] = jnp.transpose(stat[...])[: stat_t.shape[1]]

    @pl.when(below)
    def _():
        stat_copy(0).start()

    @pl.when(above)
    def _():
        stat_copy(1).start()

    own_cols = pl.ds(pl.multiple_of(me_dp * block, block), block)
    latt_ref[:, :slab] = jnp.transpose(lat_buf[1, :, own_cols])
    for step in range(1, n_dp):
        clip_copy(step).wait_recv()
        latt_ref[:, step * slab : (step + 1) * slab] = jnp.transpose(clip_buf[step - 1])

    @pl.when(above)
    def _():
        do_copy(0).wait_recv()
        stat_copy(0).wait_recv()

    @pl.when(below)
    def _():
        do_copy(1).wait_recv()
        stat_copy(1).wait_recv()

    @pl.loop(0, heads)
    def _(h):
        keys = k_hat[1, :, at(h)]
        values = v_hat[1, :, at(h)]
        queries = q_hat[:, :, at(h)].reshape(3 * slab, HD)
        upstream = do_buf[:, :, at(h)].reshape(3 * slab, HD)
        total = jnp.concatenate([stat_t[s, pl.ds(2 * h, 1), :] for s in range(3)], axis=1)
        delta = jnp.concatenate([stat_t[s, pl.ds(2 * h + 1, 1), :] for s in range(3)], axis=1)
        probs = jnp.exp(nt(keys, queries) * scale) * mask_t[...] * (1.0 / total)
        put(2, h, jnp.dot(probs.astype(jnp.bfloat16), upstream, preferred_element_type=jnp.float32))
        d_scores = (probs * (nt(values, upstream) - delta) * scale).astype(jnp.bfloat16)
        d_khat = jnp.dot(d_scores, queries, preferred_element_type=jnp.float32)
        raw = k_raw[:, at(h)]
        put(1, h, norm_back(raw, inv_rms(raw), k_gain, d_khat))

    def settle(slot, side):
        lat_copy(side).wait_send()
        do_copy(side).wait_send()
        stat_copy(side).wait_send()
        for step in range(1, n_head):
            pass_copy(slot, step).wait_send()

    @pl.when(below)
    def _():
        settle(0, 0)

    @pl.when(above)
    def _():
        settle(2, 1)

    for step in range(1, n_dp):
        clip_copy(step).wait_send()


def layer(slab_tokens, w_three, q_gain, k_gain, neighbours, upstream):
    n_dp, n_seq, n_head = (lax.axis_size(axis) for axis in ("dp", "seq", "head"))
    slab = slab_tokens.shape[0]
    three, model_width, head_width = w_three.shape
    heads = head_width // HD
    group = 3 if heads % 3 == 0 else 1
    width = group * HD
    chunks = three * heads // group
    block = model_width // n_dp
    stat_rows = -(-2 * heads // 8) * 8
    vmem = pl.BlockSpec(memory_space=pltpu.VMEM)
    anywhere = pl.BlockSpec(memory_space=pl.ANY)
    dma = pltpu.SemaphoreType.DMA
    bf16, f32 = jnp.bfloat16, jnp.float32
    return pl.pallas_call(
        functools.partial(layer_kernel, n_dp, n_seq, n_head),
        out_shape=(
            jax.ShapeDtypeStruct((slab, head_width), bf16),
            jax.ShapeDtypeStruct((chunks, slab, width), bf16),
            jax.ShapeDtypeStruct((block, n_dp * slab), bf16),
        ),
        in_specs=[anywhere, anywhere, vmem, vmem, vmem, anywhere],
        out_specs=(vmem, vmem, vmem),
        scratch_shapes=[
            pltpu.VMEM((3, slab, model_width), bf16),
            pltpu.VMEM((three, model_width, head_width), bf16),
            pltpu.VMEM((3, slab, head_width), bf16),
            pltpu.VMEM((slab, head_width), f32),
            pltpu.VMEM((slab, head_width), f32),
            pltpu.VMEM((3, slab, head_width), bf16),
            pltpu.VMEM((3, slab, head_width), bf16),
            pltpu.VMEM((3, slab, head_width), bf16),
            pltpu.VMEM((slab, 3 * slab), f32),
            pltpu.VMEM((slab, 3 * slab), f32),
            pltpu.VMEM((slab, 128), f32),
            pltpu.VMEM((3, stat_rows, slab), f32),
            pltpu.VMEM((n_dp - 1, slab, block), bf16),
            dma((2,)),
            dma((chunks,)),
            dma((2,)),
            dma((2,)),
            dma((2, n_head - 1)),
            dma((2, n_head - 1)),
            dma((2,)),
            dma((2,)),
            dma((2,)),
            dma((2,)),
            dma((n_dp - 1,)),
            dma((n_dp - 1,)),
        ],
        compiler_params=pltpu.CompilerParams(
            collective_id=1, has_side_effects=True, vmem_limit_bytes=60 * 1024 * 1024
        ),
        name="layer",
    )(slab_tokens, w_three, q_gain.reshape(1, HD), k_gain.reshape(1, HD), neighbours, upstream)


def local(latents, w_qkv, q_gain, k_gain, neighbours, grad_out):
    w_three = jnp.transpose(w_qkv, (1, 0, 2))
    attn_out, d_chunks, lat_t = layer(
        latents[0], w_three, q_gain, k_gain, neighbours, grad_out[0]
    )
    share, grad_rows = grads(d_chunks, lat_t, w_three)
    return (attn_out[None], grad_rows[None], jnp.transpose(share, (1, 0, 2)))


def solution(mesh):
    in_specs = (P("dp", "seq", None), P(None, None, "head"), P(), P(), P(), P("dp", "seq", "head"))
    out_specs = (
        P("dp", "seq", "head"),
        P("dp", ("seq", "head"), None),
        P(("dp", "seq"), None, "head"),
    )
    return jax.shard_map(local, mesh=mesh, in_specs=in_specs, out_specs=out_specs, check_vma=False)
```

time: 213 us -> 141 us (0.66)
  local copies, waits for them, and re-layouts: 59.5 us -> 3.65 us
  Pallas kernels: 88.4 us -> 136 us
  matrix products: 27.9 us -> 0 us
  starting transfers between devices: 23.7 us -> 0 us
  other arithmetic: 11.3 us -> 0 us
    pallas_call x0 -> x1, Pallas kernels: none -> 45.5 us  [layer(): pl.pallas_call(functools.partial(layer_kernel, n_dp, n_seq, n_head), out_...]
    dot_general x8 -> x0, matrix products: 27.9 us -> none  [the longest x1 6.36 us: local(): jnp.einsum('hqk,khe->qhe', d_scores, keys_wide, preferred_element_type=jn...]
    ppermute x9 -> x0, starting transfers between devices: 23.7 us -> none  [the longest x3 16.2 us: with_halo(): lax.ppermute(lax.slice_in_dim(block, block.shape[dim] - width, None, axis...]
    unnamed x45 -> x7, local copies, waits for them, and re-layouts: 22 us -> 3.65 us
    reshape x3 -> x0, local copies, waits for them, and re-layouts: 14.1 us -> none  [the longest x1 12.6 us: local(): flat_w = w_qkv.reshape(model_width, 3 * head_width)]
    dynamic_slice x9 -> x0, local copies, waits for them, and re-layouts: 8.56 us -> none  [the longest x5 8.34 us: clip_columns(): piece = lax.dynamic_slice_in_dim(slab_tokens, target * width, width, 1)]
    mul x6 -> x0, local copies, waits for them, and re-layouts: 5.3 us -> none  [the longest x1 2.31 us: local(): jnp.exp(scores_back) * reverse_allowed[None] / safe_total[..., None]]
    broadcast_in_dim x4 -> x0, local copies, waits for them, and re-layouts: 3.38 us -> none  [tile_allowed(): return jnp.repeat(jnp.repeat(block, TILE, axis=0), TILE, axis=1)]
  transfers between devices with their start and end apart: 9 -> 0, of which waited for: 0 -> 0; matrix products, arithmetic and copies ran while one was open for 24% -> 0% of each run, Pallas kernels for 0% -> 0%
where the time goes in v2:
time: 141 us; the launch traced here: 140 us
  Pallas kernels  136 us (96%)
  local copies, waits for them, and re-layouts  3.65 us (3%)
    pallas_call x1, Pallas kernels, grads(): pl.pallas_call(functools.partial(grads_kernel, n_dp, n_seq, n_head), out_...  90.5 us
    pallas_call x1, Pallas kernels, layer(): pl.pallas_call(functools.partial(layer_kernel, n_dp, n_seq, n_head), out_...  45.5 us
    unnamed x7, local copies, waits for them, and re-layouts  3.65 us

profile of v2, /device:TPU:0, one launch (start us, length us, event | category | flops | bytes accessed | tf_op | source)
XLA Modules:
  0.0 140.3 jit_solution(8617904558727892913)
XLA Ops:
  0.6 45.5 %layer.1 = (bf16[256,768]{1,0:T(8,128)(2,1)}, bf16[6,256,384]{2,1,0:T(8,128)(2,1)}, bf16[512,1024]{1,0:T(8,128)(2,1)}) custom-call(bf16[256,2048]{1,0:T(8,128)(2,1)} %bitcast.11, bf16[3,2048,768]{2,1,0:T(8,128)(2,1)} %bitcast.8, f32[1,128]{1,0:T(1,128)} %bitcast.15, f32[1,128]{1,0:T(1,128)} %bitcast.16, s32[16,9]{1,0:T(8,128)} %near_ref.1, ...), custom_call_target="tpu_custom_call" | custom-call | tf_op jit(solution)/shard_map/layer/pallas_call | solution.py:569
  46.1 0.0 copy-start.1
  46.1 90.5 %grads.1 = (f32[3,128,768]{2,1,0:T(8,128)}, bf16[128,2048]{1,0:T(8,128)(2,1)}) custom-call(bf16[6,256,384]{2,1,0:T(8,128)(2,1)} %get-tuple-element.9.dq_ref, bf16[512,1024]{1,0:T(8,128)(2,1)} %get-tuple-element.10.lat_ref, bf16[3,2048,768]{2,1,0:T(8,128)(2,1)} %bitcast.9), custom_call_target="tpu_custom_call" | custom-call | tf_op jit(solution)/shard_map/grads/pallas_call | solution.py:206
  136.7 0.0 copy-start
  136.7 0.0 copy-done.1
  136.7 0.7 copy.12
  137.4 1.9 %copy.13 = bf16[1,128,2048]{2,1,0:T(8,128)(2,1)} copy(bf16[1,128,2048]{2,1,0:T(8,128)(2,1)} %bitcast.12) | data formatting | bytes 1048576
  139.3 0.0 copy-done
  139.3 1.0 copy.14
Async XLA Ops:
  46.1 90.6 %copy-start.1 = (bf16[256,768]{1,0:T(8,128)(2,1)S(1)}, bf16[256,768]{1,0:T(8,128)(2,1)}, u32[]{:S(2)}) copy-start(bf16[256,768]{1,0:T(8,128)(2,1)} %get-tuple-element.8) | copy-start | bytes 1179652
  136.7 2.7 %copy-start = (f32[3,128,768]{2,1,0:T(8,128)S(1)}, f32[3,128,768]{2,1,0:T(8,128)}, u32[]{:S(2)}) copy-start(f32[3,128,768]{2,1,0:T(8,128)} %get-tuple-element.12) | copy-start | bytes 3538948

commit v3 on v2

--- a/solution.py
+++ b/solution.py
@@ -38,207 +38,12 @@
     )
 
 
-def grads_kernel(
-    n_dp, n_seq, n_head, dq_ref, lat_ref, w_ref, gw_ref, gx_ref,
-    gath, w_buf, part, z_send, z_recv, gx_acc, gx_recv,
-    w_sem, d_ss, d_rs, z_ss, z_rs, h_ss, h_rs,
-):
-    chunks, slab, width = dq_ref.shape
-    rows = part.shape[1]
-    half = gx_ref.shape[0]
-    me_dp = lax.axis_index("dp")
-    me_seq = lax.axis_index("seq")
-    me_head = lax.axis_index("head")
-    relay = n_dp == 4
-    parts = chunks // w_ref.shape[0]
-
-    def cols(c):
-        return pl.ds(pl.multiple_of(lax.rem(c, parts) * width, width), width)
-
-    def dp_peer(step):
-        if relay:
-            low, high = lax.rem(me_dp, 2), me_dp // 2
-            if step % 2:
-                low = 1 - low
-            if step // 2:
-                high = 1 - high
-            return {"dp": high * 2 + low}
-        return {"dp": lax.rem(me_dp + step, n_dp)}
-
-    def dp_source(step):
-        if relay:
-            return dp_peer(step)
-        return {"dp": lax.rem(me_dp + n_dp - step, n_dp)}
-
-    direct = (1, 2) if relay else tuple(range(1, n_dp))
-
-    def seq_peer(step):
-        return lax.rem(me_seq + step, n_seq)
-
-    def head_peer(step):
-        return lax.rem(me_head + step, n_head)
-
-    def w_copy(c):
-        return pltpu.make_async_copy(w_ref.at[c // parts, :, cols(c)], w_buf.at[c], w_sem.at[c])
-
-    @pl.loop(0, chunks)
-    def _(c):
-        w_copy(c).start()
-
-    barrier = pltpu.get_barrier_semaphore()
-    greeted = 0
-    for step in direct:
-        pl.semaphore_signal(barrier, inc=1, device_id=dp_source(step), device_id_type=MESH)
-        greeted += 1
-    for step in range(1, n_seq):
-        pl.semaphore_signal(
-            barrier, inc=1, device_id={"seq": seq_peer(step)}, device_id_type=MESH
-        )
-        greeted += 1
-    for step in range(1, n_head):
-        pl.semaphore_signal(
-            barrier, inc=1, device_id={"head": head_peer(step)}, device_id_type=MESH
-        )
-        greeted += 1
-    pl.semaphore_wait(barrier, greeted)
-
-    def dp_copy(c, step):
-        return remote(
-            dq_ref.at[c], gath.at[c, step - 1],
-            d_ss.at[c, step - 1], d_rs.at[c, step - 1], dp_peer(step),
-        )
-
-    def relay_copy(c, via, onward):
-        return remote(
-            gath.at[c, via - 1], gath.at[c, 2], d_ss.at[c, 2], d_rs.at[c, 2], dp_peer(onward)
-        )
-
-    @pl.loop(0, chunks)
-    def _(c):
-        for step in direct:
-            dp_copy(c, step).start()
-
-    gx_acc[...] = jnp.zeros_like(gx_acc)
-
-    def z_copy(c, step):
-        return remote(
-            z_send.at[c, seq_peer(step)], z_recv.at[c, step - 1],
-            z_ss.at[c, step - 1], z_rs.at[c, step - 1], {"seq": seq_peer(step)},
-        )
-
-    def input_share(c):
-        w_copy(c).wait()
-        gx_acc[...] += lax.dot_general(
-            dq_ref[c], w_buf[c], (((1,), (1,)), ((), ())), preferred_element_type=jnp.float32
-        )
-
-    def weight_share(c):
-        if relay:
-            relay_copy(c, 1, 2).wait_recv()
-        others = gath[c].reshape((n_dp - 1) * slab, width)
-        product = jnp.dot(lat_ref[:, :slab], dq_ref[c], preferred_element_type=jnp.float32)
-        product += jnp.dot(lat_ref[:, slab:], others, preferred_element_type=jnp.float32)
-        product = product.reshape(n_seq, rows, width)
-        part[...] = product
-        z_send[c] = product.astype(jnp.bfloat16)
-        for step in range(n_seq - 1, 0, -1):
-            z_copy(c, step).start()
-        gw_ref[c // parts, :, cols(c)] = part[me_seq]
-
-    @pl.loop(0, chunks)
-    def _(c):
-        for step in direct:
-            dp_copy(c, step).wait_recv()
-        if relay:
-            @pl.when(lax.rem(c, 2) == 0)
-            def _():
-                relay_copy(c, 1, 2).start()
-
-            @pl.when(lax.rem(c, 2) == 1)
-            def _():
-                relay_copy(c, 2, 1).start()
-
-        input_share(c)
-
-        @pl.when(c > 0)
-        def _():
-            weight_share(c - 1)
-
-    def h_copy(step):
-        return remote(
-            gx_acc.at[pl.ds(pl.multiple_of(head_peer(step) * half, half), half)],
-            gx_recv.at[step - 1], h_ss.at[step - 1], h_rs.at[step - 1],
-            {"head": head_peer(step)},
-        )
-
-    for step in range(1, n_head):
-        h_copy(step).start()
-    weight_share(chunks - 1)
-    for step in range(1, n_head):
-        h_copy(step).wait()
-    total = gx_acc[pl.ds(pl.multiple_of(me_head * half, half), half)]
-    for step in range(1, n_head):
-        total = total + gx_recv[step - 1]
-    gx_ref[...] = total.astype(gx_ref.dtype)
-
-    @pl.loop(0, chunks)
-    def _(c):
-        for step in range(1, n_seq):
-            z_copy(c, step).wait()
-        share = gw_ref[c // parts, :, cols(c)]
-        for step in range(1, n_seq):
-            share = share + z_recv[c, step - 1].astype(jnp.float32)
-        gw_ref[c // parts, :, cols(c)] = share
-        for step in direct:
-            dp_copy(c, step).wait_send()
-        if relay:
-            relay_copy(c, 1, 2).wait_send()
-
-
-def grads(d_chunks, lat_t, w_three):
-    n_dp, n_seq, n_head = (lax.axis_size(axis) for axis in ("dp", "seq", "head"))
-    chunks, slab, width = d_chunks.shape
-    three, model_width, head_width = w_three.shape
-    rows = model_width // (n_dp * n_seq)
-    half = slab // n_head
-    vmem = pl.BlockSpec(memory_space=pltpu.VMEM)
-    dma = pltpu.SemaphoreType.DMA
-    return pl.pallas_call(
-        functools.partial(grads_kernel, n_dp, n_seq, n_head),
-        out_shape=(
-            jax.ShapeDtypeStruct((three, rows, head_width), jnp.float32),
-            jax.ShapeDtypeStruct((half, model_width), jnp.bfloat16),
-        ),
-        in_specs=[vmem, vmem, pl.BlockSpec(memory_space=pl.ANY)],
-        out_specs=(vmem, vmem),
-        scratch_shapes=[
-            pltpu.VMEM((chunks, n_dp - 1, slab, width), jnp.bfloat16),
-            pltpu.VMEM((chunks, model_width, width), jnp.bfloat16),
-            pltpu.VMEM((n_seq, rows, width), jnp.float32),
-            pltpu.VMEM((chunks, n_seq, rows, width), jnp.bfloat16),
-            pltpu.VMEM((chunks, n_seq - 1, rows, width), jnp.bfloat16),
-            pltpu.VMEM((slab, model_width), jnp.float32),
-            pltpu.VMEM((n_head - 1, half, model_width), jnp.float32),
-            dma((chunks,)),
-            dma((chunks, n_dp - 1)),
-            dma((chunks, n_dp - 1)),
-            dma((chunks, n_seq - 1)),
-            dma((chunks, n_seq - 1)),
-            dma((n_head - 1,)),
-            dma((n_head - 1,)),
-        ],
-        compiler_params=pltpu.CompilerParams(
-            collective_id=0, has_side_effects=True, vmem_limit_bytes=60 * 1024 * 1024
-        ),
-        name="grads",
-    )(d_chunks, lat_t, w_three)
-
-
 def layer_kernel(
     n_dp, n_seq, n_head, lat_ref, w_ref, qg_ref, kg_ref, near_ref, do_ref,
-    out_ref, d_ref, latt_ref,
-    lat_buf, w_buf, do_buf, q_raw, k_raw, q_hat, k_hat, v_hat, mask, mask_t, stat, stat_t, clip_buf,
+    out_ref, gw_ref, gx_ref,
+    d_ref, latt_ref, gath, part, z_send, z_recv, gx_acc, gx_recv, lat_buf, w_buf, do_buf, q_raw, k_raw, q_hat, k_hat, v_hat, mask, mask_t, stat, stat_t, clip_buf,
     l_sem, w_sem, a_ss, a_rs, f_ss, f_rs, o_ss, o_rs, s_ss, s_rs, c_ss, c_rs,
+    d_ss, d_rs, z_ss, z_rs, h_ss, h_rs,
 ):
     three, model_width, head_width = w_ref.shape
     slab = lat_ref.shape[0]
@@ -288,16 +93,14 @@
 
     own_do.start()
 
+    def seq_peer(step):
+        return lax.rem(me_seq + step, n_seq)
+
     barrier = pltpu.get_barrier_semaphore()
-
-    @pl.when(below)
-    def _():
-        pl.semaphore_signal(barrier, inc=1, device_id={"seq": me_seq - 1}, device_id_type=MESH)
-
-    @pl.when(above)
-    def _():
-        pl.semaphore_signal(barrier, inc=1, device_id={"seq": me_seq + 1}, device_id_type=MESH)
-
+    for step in range(1, n_seq):
+        pl.semaphore_signal(
+            barrier, inc=1, device_id={"seq": seq_peer(step)}, device_id_type=MESH
+        )
     for step in range(1, n_dp):
         pl.semaphore_signal(
             barrier, inc=1, device_id={"dp": dp_peer(step, -1)}, device_id_type=MESH
@@ -306,8 +109,7 @@
         pl.semaphore_signal(
             barrier, inc=1, device_id={"head": head_peer(step, -1)}, device_id_type=MESH
         )
-    sides = jnp.minimum(me_seq, 1) + jnp.minimum(n_seq - 1 - me_seq, 1)
-    pl.semaphore_wait(barrier, n_dp - 1 + n_head - 1 + sides)
+    pl.semaphore_wait(barrier, n_seq - 1 + n_dp - 1 + n_head - 1)
 
     my_rows = pl.ds(pl.multiple_of(me_head * half, half), half)
 
@@ -465,8 +267,71 @@
     def nt(a, b):
         return lax.dot_general(a, b, (((1,), (1,)), ((), ())), preferred_element_type=jnp.float32)
 
-    def put(kind, h, value):
-        d_ref[kind * parts + h // group, :, at(lax.rem(h, group))] = value.astype(jnp.bfloat16)
+    def put(position, h, value):
+        d_ref[position, :, at(lax.rem(h, group))] = value.astype(jnp.bfloat16)
+
+    def place(position):
+        late = jnp.maximum(position - parts, 0)
+        is_late = jnp.where(position >= parts, 1, 0)
+        kind = is_late * (1 + lax.rem(late, 2))
+        p = is_late * (late // 2) + (1 - is_late) * position
+        return kind, cols(p)
+
+    relay = n_dp == 4
+    direct = (1, 2) if relay else tuple(range(1, n_dp))
+    rows = gw_ref.shape[1]
+
+    def dp_copy(c, step):
+        return remote(
+            d_ref.at[c], gath.at[c, step - 1],
+            d_ss.at[c, step - 1], d_rs.at[c, step - 1], {"dp": dp_peer(step)},
+        )
+
+    def relay_copy(c, via, onward):
+        return remote(
+            gath.at[c, via - 1], gath.at[c, 2],
+            d_ss.at[c, 2], d_rs.at[c, 2], {"dp": dp_peer(onward)},
+        )
+
+    def z_copy(c, step):
+        return remote(
+            z_send.at[c, seq_peer(step)], z_recv.at[c, step - 1],
+            z_ss.at[c, step - 1], z_rs.at[c, step - 1], {"seq": seq_peer(step)},
+        )
+
+    def send_own(c):
+        for step in direct:
+            dp_copy(c, step).start()
+
+    def pass_on(c):
+        for step in direct:
+            dp_copy(c, step).wait_recv()
+        if relay:
+            @pl.when(lax.rem(c, 2) == 0)
+            def _():
+                relay_copy(c, 1, 2).start()
+
+            @pl.when(lax.rem(c, 2) == 1)
+            def _():
+                relay_copy(c, 2, 1).start()
+
+    def input_share(c):
+        kind, where = place(c)
+        gx_acc[...] += nt(d_ref[c], w_buf[kind, :, where])
+
+    def weight_share(c):
+        if relay:
+            relay_copy(c, 1, 2).wait_recv()
+        others = gath[c].reshape((n_dp - 1) * slab, width)
+        product = jnp.dot(latt_ref[:, :slab], d_ref[c], preferred_element_type=jnp.float32)
+        product += jnp.dot(latt_ref[:, slab:], others, preferred_element_type=jnp.float32)
+        product = product.reshape(n_seq, rows, width)
+        part[...] = product
+        z_send[c] = product.astype(jnp.bfloat16)
+        for step in range(n_seq - 1, 0, -1):
+            z_copy(c, step).start()
+        kind, where = place(c)
+        gw_ref[kind, :, where] = part[me_seq]
 
     own_do.wait()
     lanes = lax.broadcasted_iota(jnp.int32, (slab, 128), 1)
@@ -488,9 +353,13 @@
         d_scores = (probs * (d_probs - row_delta) * scale).astype(jnp.bfloat16)
         d_qhat = jnp.dot(d_scores, keys, preferred_element_type=jnp.float32)
         raw = q_raw[:, at(h)]
-        put(0, h, norm_back(raw, inv_rms(raw), q_gain, d_qhat))
+        put(h // group, h, norm_back(raw, inv_rms(raw), q_gain, d_qhat))
         rows = jnp.where(lanes == 2 * h, row_total, stat[...])
         stat[...] = jnp.where(lanes == 2 * h + 1, row_delta, rows)
+
+        @pl.when(lax.rem(h, group) == group - 1)
+        def _():
+            send_own(h // group)
 
     stat_t[1] = jnp.transpose(stat[...])[: stat_t.shape[1]]
 
@@ -518,8 +387,9 @@
         do_copy(1).wait_recv()
         stat_copy(1).wait_recv()
 
-    @pl.loop(0, heads)
-    def _(h):
+    gx_acc[...] = jnp.zeros_like(gx_acc)
+
+    def reverse(h):
         keys = k_hat[1, :, at(h)]
         values = v_hat[1, :, at(h)]
         queries = q_hat[:, :, at(h)].reshape(3 * slab, HD)
@@ -527,11 +397,65 @@
         total = jnp.concatenate([stat_t[s, pl.ds(2 * h, 1), :] for s in range(3)], axis=1)
         delta = jnp.concatenate([stat_t[s, pl.ds(2 * h + 1, 1), :] for s in range(3)], axis=1)
         probs = jnp.exp(nt(keys, queries) * scale) * mask_t[...] * (1.0 / total)
-        put(2, h, jnp.dot(probs.astype(jnp.bfloat16), upstream, preferred_element_type=jnp.float32))
+        late = parts + 2 * (h // group)
+        put(late + 1, h, jnp.dot(probs.astype(jnp.bfloat16), upstream, preferred_element_type=jnp.float32))
         d_scores = (probs * (nt(values, upstream) - delta) * scale).astype(jnp.bfloat16)
         d_khat = jnp.dot(d_scores, queries, preferred_element_type=jnp.float32)
         raw = k_raw[:, at(h)]
-        put(1, h, norm_back(raw, inv_rms(raw), k_gain, d_khat))
+        put(late, h, norm_back(raw, inv_rms(raw), k_gain, d_khat))
+
+    @pl.loop(0, chunks)
+    def _(tick):
+        @pl.when(tick > 0)
+        def _():
+            weight_share(tick - 1)
+
+        @pl.when(tick < parts)
+        def _():
+            @pl.loop(0, group)
+            def _(h):
+                reverse(tick * group + h)
+
+        pass_on(tick)
+
+        @pl.when(tick < chunks - parts)
+        def _():
+            send_own(tick + parts)
+
+        input_share(tick)
+
+    share = gx_ref.shape[0]
+
+    def h_copy(step):
+        peer = head_peer(step)
+        return remote(
+            gx_acc.at[pl.ds(pl.multiple_of(peer * share, share), share)],
+            gx_recv.at[step - 1], h_ss.at[step - 1], h_rs.at[step - 1], {"head": peer},
+        )
+
+    for step in range(1, n_head):
+        h_copy(step).start()
+    weight_share(chunks - 1)
+    for step in range(1, n_head):
+        h_copy(step).wait()
+    total = gx_acc[pl.ds(pl.multiple_of(me_head * share, share), share)]
+    for step in range(1, n_head):
+        total = total + gx_recv[step - 1]
+    gx_ref[...] = total.astype(gx_ref.dtype)
+
+    @pl.loop(0, chunks)
+    def _(c):
+        for step in range(1, n_seq):
+            z_copy(c, step).wait()
+        kind, where = place(c)
+        summed = gw_ref[kind, :, where]
+        for step in range(1, n_seq):
+            summed = summed + z_recv[c, step - 1].astype(jnp.float32)
+        gw_ref[kind, :, where] = summed
+        for step in direct:
+            dp_copy(c, step).wait_send()
+        if relay:
+            relay_copy(c, 1, 2).wait_send()
 
     def settle(slot, side):
         lat_copy(side).wait_send()
@@ -561,6 +485,8 @@
     width = group * HD
     chunks = three * heads // group
     block = model_width // n_dp
+    rows = block // n_seq
+    share = slab // n_head
     stat_rows = -(-2 * heads // 8) * 8
     vmem = pl.BlockSpec(memory_space=pltpu.VMEM)
     anywhere = pl.BlockSpec(memory_space=pl.ANY)
@@ -570,12 +496,20 @@
         functools.partial(layer_kernel, n_dp, n_seq, n_head),
         out_shape=(
             jax.ShapeDtypeStruct((slab, head_width), bf16),
-            jax.ShapeDtypeStruct((chunks, slab, width), bf16),
-            jax.ShapeDtypeStruct((block, n_dp * slab), bf16),
+            jax.ShapeDtypeStruct((three, rows, head_width), f32),
+            jax.ShapeDtypeStruct((share, model_width), bf16),
         ),
         in_specs=[anywhere, anywhere, vmem, vmem, vmem, anywhere],
         out_specs=(vmem, vmem, vmem),
         scratch_shapes=[
+            pltpu.VMEM((chunks, slab, width), bf16),
+            pltpu.VMEM((block, n_dp * slab), bf16),
+            pltpu.VMEM((chunks, n_dp - 1, slab, width), bf16),
+            pltpu.VMEM((n_seq, rows, width), f32),
+            pltpu.VMEM((chunks, n_seq, rows, width), bf16),
+            pltpu.VMEM((chunks, n_seq - 1, rows, width), bf16),
+            pltpu.VMEM((slab, model_width), f32),
+            pltpu.VMEM((n_head - 1, share, model_width), f32),
             pltpu.VMEM((3, slab, model_width), bf16),
             pltpu.VMEM((three, model_width, head_width), bf16),
             pltpu.VMEM((3, slab, head_width), bf16),
@@ -601,9 +535,15 @@
             dma((2,)),
             dma((n_dp - 1,)),
             dma((n_dp - 1,)),
+            dma((chunks, n_dp - 1)),
+            dma((chunks, n_dp - 1)),
+            dma((chunks, n_seq - 1)),
+            dma((chunks, n_seq - 1)),
+            dma((n_head - 1,)),
+            dma((n_head - 1,)),
         ],
         compiler_params=pltpu.CompilerParams(
-            collective_id=1, has_side_effects=True, vmem_limit_bytes=60 * 1024 * 1024
+            collective_id=0, has_side_effects=True, vmem_limit_bytes=60 * 1024 * 1024
         ),
         name="layer",
     )(slab_tokens, w_three, q_gain.reshape(1, HD), k_gain.reshape(1, HD), neighbours, upstream)
@@ -611,11 +551,10 @@
 
 def local(latents, w_qkv, q_gain, k_gain, neighbours, grad_out):
     w_three = jnp.transpose(w_qkv, (1, 0, 2))
-    attn_out, d_chunks, lat_t = layer(
+    attn_out, grad_w, grad_x = layer(
         latents[0], w_three, q_gain, k_gain, neighbours, grad_out[0]
     )
-    share, grad_rows = grads(d_chunks, lat_t, w_three)
-    return (attn_out[None], grad_rows[None], jnp.transpose(share, (1, 0, 2)))
+    return (attn_out[None], grad_x[None], jnp.transpose(grad_w, (1, 0, 2)))
 
 
 def solution(mesh):

time: 141 us -> 110 us (0.78)
  Pallas kernels: 136 us -> 105 us
    pallas_call x1 -> x0, Pallas kernels: 90.5 us -> none  [grads(): pl.pallas_call(functools.partial(grads_kernel, n_dp, n_seq, n_head), out_...]
    pallas_call x1, Pallas kernels: 45.5 us -> 105 us  [layer(): pl.pallas_call(functools.partial(layer_kernel, n_dp, n_seq, n_head), out_...]
    unnamed x7 -> x5, local copies, waits for them, and re-layouts: 3.65 us -> 4.76 us
where the time goes in v3:
time: 110 us
  Pallas kernels  105 us (95%)
  local copies, waits for them, and re-layouts  4.76 us (4%)
    pallas_call x1, Pallas kernels, layer(): pl.pallas_call(functools.partial(layer_kernel, n_dp, n_seq, n_head), out_...  105 us
    unnamed x5, local copies, waits for them, and re-layouts  4.76 us

profile of v3, /device:TPU:0, one launch (start us, length us, event | category | flops | bytes accessed | tf_op | source)
XLA Modules:
  0.0 110.0 jit_solution(10251933322969211758)
XLA Ops:
  0.6 104.6 %layer.1 = (bf16[256,768]{1,0:T(8,128)(2,1)}, f32[3,128,768]{2,1,0:T(8,128)}, bf16[128,2048]{1,0:T(8,128)(2,1)}) custom-call(bf16[256,2048]{1,0:T(8,128)(2,1)} %bitcast.10, bf16[3,2048,768]{2,1,0:T(8,128)(2,1)} %bitcast.8, f32[1,128]{1,0:T(1,128)} %bitcast.14, f32[1,128]{1,0:T(1,128)} %bitcast.15, s32[16,9]{1,0:T(8,128)} %near_ref.1, bf16[256,768]{1,0:T(8,128)(2,1)} %bitcast.12), custom_call_target="tpu_custom_call" | custom-call | tf_op jit(solution)/shard_map/layer/pallas_call | solution.py:495
  105.3 0.0 copy-start
  105.3 1.9 %copy.12 = bf16[1,256,768]{2,1,0:T(8,128)(2,1)} copy(bf16[1,256,768]{2,1,0:T(8,128)(2,1)} %bitcast.13) | data formatting | bytes 786432
  107.1 1.9 %copy.13 = bf16[1,128,2048]{2,1,0:T(8,128)(2,1)} copy(bf16[1,128,2048]{2,1,0:T(8,128)(2,1)} %bitcast.11) | data formatting | bytes 1048576
  109.0 0.0 copy-done
  109.0 1.0 copy.14
Async XLA Ops:
  105.3 3.8 %copy-start = (f32[3,128,768]{2,1,0:T(8,128)S(1)}, f32[3,128,768]{2,1,0:T(8,128)}, u32[]{:S(2)}) copy-start(f32[3,128,768]{2,1,0:T(8,128)} %get-tuple-element.8) | copy-start | bytes 3538948

commit v4 on v3

--- a/solution.py
+++ b/solution.py
@@ -41,7 +41,7 @@
 def layer_kernel(
     n_dp, n_seq, n_head, lat_ref, w_ref, qg_ref, kg_ref, near_ref, do_ref,
     out_ref, gw_ref, gx_ref,
-    d_ref, latt_ref, gath, part, z_send, z_recv, gx_acc, gx_recv, lat_buf, w_buf, do_buf, q_raw, k_raw, q_hat, k_hat, v_hat, mask, mask_t, stat, stat_t, clip_buf,
+    d_ref, latt_ref, gath, part, flow, gx_acc, gx_recv, lat_buf, w_buf, do_buf, q_raw, k_raw, q_hat, k_hat, v_hat, mask, mask_t, stat, stat_t, clip_buf,
     l_sem, w_sem, a_ss, a_rs, f_ss, f_rs, o_ss, o_rs, s_ss, s_rs, c_ss, c_rs,
     d_ss, d_rs, z_ss, z_rs, h_ss, h_rs,
 ):
@@ -93,14 +93,16 @@
 
     own_do.start()
 
-    def seq_peer(step):
-        return lax.rem(me_seq + step, n_seq)
-
     barrier = pltpu.get_barrier_semaphore()
-    for step in range(1, n_seq):
-        pl.semaphore_signal(
-            barrier, inc=1, device_id={"seq": seq_peer(step)}, device_id_type=MESH
-        )
+
+    @pl.when(below)
+    def _():
+        pl.semaphore_signal(barrier, inc=1, device_id={"seq": me_seq - 1}, device_id_type=MESH)
+
+    @pl.when(above)
+    def _():
+        pl.semaphore_signal(barrier, inc=1, device_id={"seq": me_seq + 1}, device_id_type=MESH)
+
     for step in range(1, n_dp):
         pl.semaphore_signal(
             barrier, inc=1, device_id={"dp": dp_peer(step, -1)}, device_id_type=MESH
@@ -109,7 +111,8 @@
         pl.semaphore_signal(
             barrier, inc=1, device_id={"head": head_peer(step, -1)}, device_id_type=MESH
         )
-    pl.semaphore_wait(barrier, n_seq - 1 + n_dp - 1 + n_head - 1)
+    sides = jnp.minimum(me_seq, 1) + jnp.minimum(n_seq - 1 - me_seq, 1)
+    pl.semaphore_wait(barrier, n_dp - 1 + n_head - 1 + sides)
 
     my_rows = pl.ds(pl.multiple_of(me_head * half, half), half)
 
@@ -293,11 +296,36 @@
             d_ss.at[c, 2], d_rs.at[c, 2], {"dp": dp_peer(onward)},
         )
 
-    def z_copy(c, step):
-        return remote(
-            z_send.at[c, seq_peer(step)], z_recv.at[c, step - 1],
-            z_ss.at[c, step - 1], z_rs.at[c, step - 1], {"seq": seq_peer(step)},
-        )
+    def hop(side, c, t):
+        peer = lax.rem(me_seq + n_seq + 1 - 2 * side, n_seq)
+        return remote(
+            flow.at[side, c, t], flow.at[side, c, t],
+            z_ss.at[side, c, t], z_rs.at[side, c, t], {"seq": peer},
+        )
+
+    fed = (below, above)
+
+    def onward(side, t):
+        return t < me_seq if side else t > me_seq
+
+    def stage(side, c):
+        @pl.loop(0, n_seq)
+        def _(turn):
+            t = turn if side else n_seq - 1 - turn
+
+            @pl.when(onward(side, t))
+            def _():
+                @pl.when(fed[side])
+                def _():
+                    hop(side, c, t).wait_recv()
+                    summed = part[c, t] + flow[side, c, t].astype(jnp.float32)
+                    flow[side, c, t] = summed.astype(jnp.bfloat16)
+
+                @pl.when(jnp.logical_not(fed[side]))
+                def _():
+                    flow[side, c, t] = part[c, t].astype(jnp.bfloat16)
+
+                hop(side, c, t).start()
 
     def send_own(c):
         for step in direct:
@@ -325,13 +353,7 @@
         others = gath[c].reshape((n_dp - 1) * slab, width)
         product = jnp.dot(latt_ref[:, :slab], d_ref[c], preferred_element_type=jnp.float32)
         product += jnp.dot(latt_ref[:, slab:], others, preferred_element_type=jnp.float32)
-        product = product.reshape(n_seq, rows, width)
-        part[...] = product
-        z_send[c] = product.astype(jnp.bfloat16)
-        for step in range(n_seq - 1, 0, -1):
-            z_copy(c, step).start()
-        kind, where = place(c)
-        gw_ref[kind, :, where] = part[me_seq]
+        part[c] = product.reshape(n_seq, rows, width)
 
     own_do.wait()
     lanes = lax.broadcasted_iota(jnp.int32, (slab, 128), 1)
@@ -404,11 +426,28 @@
         raw = k_raw[:, at(h)]
         put(late, h, norm_back(raw, inv_rms(raw), k_gain, d_khat))
 
-    @pl.loop(0, chunks)
+    share = gx_ref.shape[0]
+
+    def h_copy(step):
+        peer = head_peer(step)
+        return remote(
+            gx_acc.at[pl.ds(pl.multiple_of(peer * share, share), share)],
+            gx_recv.at[step - 1], h_ss.at[step - 1], h_rs.at[step - 1], {"head": peer},
+        )
+
+    @pl.loop(0, chunks + n_seq - 1)
     def _(tick):
-        @pl.when(tick > 0)
+        @pl.when((tick > 0) & (tick <= chunks))
         def _():
             weight_share(tick - 1)
+
+        for side in range(2):
+            lag = n_seq - 1 - me_seq if side else me_seq
+            c = tick - 1 - lag
+
+            @pl.when((c >= 0) & (c < chunks))
+            def _():
+                stage(side, c)
 
         @pl.when(tick < parts)
         def _():
@@ -416,26 +455,22 @@
             def _(h):
                 reverse(tick * group + h)
 
-        pass_on(tick)
-
-        @pl.when(tick < chunks - parts)
+        @pl.when(tick < chunks)
         def _():
-            send_own(tick + parts)
-
-        input_share(tick)
-
-    share = gx_ref.shape[0]
-
-    def h_copy(step):
-        peer = head_peer(step)
-        return remote(
-            gx_acc.at[pl.ds(pl.multiple_of(peer * share, share), share)],
-            gx_recv.at[step - 1], h_ss.at[step - 1], h_rs.at[step - 1], {"head": peer},
-        )
-
-    for step in range(1, n_head):
-        h_copy(step).start()
-    weight_share(chunks - 1)
+            pass_on(tick)
+
+            @pl.when(tick < chunks - parts)
+            def _():
+                send_own(tick + parts)
+
+            input_share(tick)
+
+        @pl.when(tick == chunks - 1)
+        def _():
+            for step in range(1, n_head):
+                h_copy(step).start()
+
+
     for step in range(1, n_head):
         h_copy(step).wait()
     total = gx_acc[pl.ds(pl.multiple_of(me_head * share, share), share)]
@@ -445,13 +480,20 @@
 
     @pl.loop(0, chunks)
     def _(c):
-        for step in range(1, n_seq):
-            z_copy(c, step).wait()
         kind, where = place(c)
-        summed = gw_ref[kind, :, where]
-        for step in range(1, n_seq):
-            summed = summed + z_recv[c, step - 1].astype(jnp.float32)
-        gw_ref[kind, :, where] = summed
+        gw_ref[kind, :, where] = part[c, me_seq]
+        for side in range(2):
+            @pl.when(fed[side])
+            def _():
+                hop(side, c, me_seq).wait_recv()
+                gw_ref[kind, :, where] += flow[side, c, me_seq].astype(jnp.float32)
+
+            @pl.loop(0, n_seq)
+            def _(t):
+                @pl.when(onward(side, t))
+                def _():
+                    hop(side, c, t).wait_send()
+
         for step in direct:
             dp_copy(c, step).wait_send()
         if relay:
@@ -505,9 +547,8 @@
             pltpu.VMEM((chunks, slab, width), bf16),
             pltpu.VMEM((block, n_dp * slab), bf16),
             pltpu.VMEM((chunks, n_dp - 1, slab, width), bf16),
-            pltpu.VMEM((n_seq, rows, width), f32),
-            pltpu.VMEM((chunks, n_seq, rows, width), bf16),
-            pltpu.VMEM((chunks, n_seq - 1, rows, width), bf16),
+            pltpu.VMEM((chunks, n_seq, rows, width), f32),
+            pltpu.VMEM((2, chunks, n_seq, rows, width), bf16),
             pltpu.VMEM((slab, model_width), f32),
             pltpu.VMEM((n_head - 1, share, model_width), f32),
             pltpu.VMEM((3, slab, model_width), bf16),
@@ -537,8 +578,8 @@
             dma((n_dp - 1,)),
             dma((chunks, n_dp - 1)),
             dma((chunks, n_dp - 1)),
-            dma((chunks, n_seq - 1)),
-            dma((chunks, n_seq - 1)),
+            dma((2, chunks, n_seq)),
+            dma((2, chunks, n_seq)),
             dma((n_head - 1,)),
             dma((n_head - 1,)),
         ],

time: 110 us -> 108 us (0.982)
  Pallas kernels: 105 us -> 102 us
    pallas_call x1, Pallas kernels: 105 us -> 102 us  [layer(): pl.pallas_call(functools.partial(layer_kernel, n_dp, n_seq, n_head), out_...]
where the time goes in v4:
time: 108 us; the launch traced here: 107 us
  Pallas kernels  102 us (94%)
  local copies, waits for them, and re-layouts  4.76 us (4%)
    pallas_call x1, Pallas kernels, layer(): pl.pallas_call(functools.partial(layer_kernel, n_dp, n_seq, n_head), out_...  102 us
    unnamed x5, local copies, waits for them, and re-layouts  4.76 us

profile of v4, /device:TPU:0, one launch (start us, length us, event | category | flops | bytes accessed | tf_op | source)
XLA Modules:
  0.0 107.3 jit_solution(16278021143163660463)
XLA Ops:
  0.6 101.9 %layer.1 = (bf16[256,768]{1,0:T(8,128)(2,1)}, f32[3,128,768]{2,1,0:T(8,128)}, bf16[128,2048]{1,0:T(8,128)(2,1)}) custom-call(bf16[256,2048]{1,0:T(8,128)(2,1)} %bitcast.10, bf16[3,2048,768]{2,1,0:T(8,128)(2,1)} %bitcast.8, f32[1,128]{1,0:T(1,128)} %bitcast.14, f32[1,128]{1,0:T(1,128)} %bitcast.15, s32[16,9]{1,0:T(8,128)} %near_ref.1, bf16[256,768]{1,0:T(8,128)(2,1)} %bitcast.12), custom_call_target="tpu_custom_call" | custom-call | tf_op jit(solution)/shard_map/layer/pallas_call | solution.py:537
  102.5 0.0 copy-start
  102.6 1.9 %copy.12 = bf16[1,256,768]{2,1,0:T(8,128)(2,1)} copy(bf16[1,256,768]{2,1,0:T(8,128)(2,1)} %bitcast.13) | data formatting | bytes 786432
  104.4 1.9 %copy.13 = bf16[1,128,2048]{2,1,0:T(8,128)(2,1)} copy(bf16[1,128,2048]{2,1,0:T(8,128)(2,1)} %bitcast.11) | data formatting | bytes 1048576
  106.3 0.0 copy-done
  106.3 1.0 copy.14
Async XLA Ops:
  102.5 3.8 %copy-start = (f32[3,128,768]{2,1,0:T(8,128)S(1)}, f32[3,128,768]{2,1,0:T(8,128)}, u32[]{:S(2)}) copy-start(f32[3,128,768]{2,1,0:T(8,128)} %get-tuple-element.8) | copy-start | bytes 3538948

commit v5 on v4

--- a/solution.py
+++ b/solution.py
@@ -399,16 +399,6 @@
         clip_copy(step).wait_recv()
         latt_ref[:, step * slab : (step + 1) * slab] = jnp.transpose(clip_buf[step - 1])
 
-    @pl.when(above)
-    def _():
-        do_copy(0).wait_recv()
-        stat_copy(0).wait_recv()
-
-    @pl.when(below)
-    def _():
-        do_copy(1).wait_recv()
-        stat_copy(1).wait_recv()
-
     gx_acc[...] = jnp.zeros_like(gx_acc)
 
     def reverse(h):
@@ -437,6 +427,14 @@
 
     @pl.loop(0, chunks + n_seq - 1)
     def _(tick):
+        @pl.when(tick < chunks)
+        def _():
+            pass_on(tick)
+
+        @pl.when((tick >= parts) & (tick < chunks - parts))
+        def _():
+            send_own(tick + parts)
+
         @pl.when((tick > 0) & (tick <= chunks))
         def _():
             weight_share(tick - 1)
@@ -449,20 +447,26 @@
             def _():
                 stage(side, c)
 
+        @pl.when((tick == 0) & above)
+        def _():
+            do_copy(0).wait_recv()
+            stat_copy(0).wait_recv()
+
+        @pl.when((tick == 0) & below)
+        def _():
+            do_copy(1).wait_recv()
+            stat_copy(1).wait_recv()
+
         @pl.when(tick < parts)
         def _():
             @pl.loop(0, group)
             def _(h):
                 reverse(tick * group + h)
 
+            send_own(tick + parts)
+
         @pl.when(tick < chunks)
         def _():
-            pass_on(tick)
-
-            @pl.when(tick < chunks - parts)
-            def _():
-                send_own(tick + parts)
-
             input_share(tick)
 
         @pl.when(tick == chunks - 1)

time: 108 us -> 101 us (0.935)
  Pallas kernels: 102 us -> 95.1 us
    pallas_call x1, Pallas kernels: 102 us -> 95.1 us  [layer(): pl.pallas_call(functools.partial(layer_kernel, n_dp, n_seq, n_head), out_...]
where the time goes in v5:
time: 101 us
  Pallas kernels  95.1 us (94%)
  local copies, waits for them, and re-layouts  4.76 us (5%)
    pallas_call x1, Pallas kernels, layer(): pl.pallas_call(functools.partial(layer_kernel, n_dp, n_seq, n_head), out_...  95.1 us
    unnamed x5, local copies, waits for them, and re-layouts  4.76 us

profile of v5, /device:TPU:0, one launch (start us, length us, event | category | flops | bytes accessed | tf_op | source)
XLA Modules:
  0.0 100.5 jit_solution(16258704145807310652)
XLA Ops:
  0.6 95.1 %layer.1 = (bf16[256,768]{1,0:T(8,128)(2,1)}, f32[3,128,768]{2,1,0:T(8,128)}, bf16[128,2048]{1,0:T(8,128)(2,1)}) custom-call(bf16[256,2048]{1,0:T(8,128)(2,1)} %bitcast.10, bf16[3,2048,768]{2,1,0:T(8,128)(2,1)} %bitcast.8, f32[1,128]{1,0:T(1,128)} %bitcast.14, f32[1,128]{1,0:T(1,128)} %bitcast.15, s32[16,9]{1,0:T(8,128)} %near_ref.1, bf16[256,768]{1,0:T(8,128)(2,1)} %bitcast.12), custom_call_target="tpu_custom_call" | custom-call | tf_op jit(solution)/shard_map/layer/pallas_call | solution.py:541
  95.8 0.0 copy-start
  95.8 1.9 %copy.12 = bf16[1,256,768]{2,1,0:T(8,128)(2,1)} copy(bf16[1,256,768]{2,1,0:T(8,128)(2,1)} %bitcast.13) | data formatting | bytes 786432
  97.6 1.9 %copy.13 = bf16[1,128,2048]{2,1,0:T(8,128)(2,1)} copy(bf16[1,128,2048]{2,1,0:T(8,128)(2,1)} %bitcast.11) | data formatting | bytes 1048576
  99.5 0.0 copy-done
  99.5 1.0 %copy.14 = f32[128,3,768]{2,0,1:T(8,128)} copy(f32[128,3,768]{2,0,1:T(8,128)S(1)} %bitcast.9) | data formatting | bytes 2359296
Async XLA Ops:
  95.8 3.8 %copy-start = (f32[3,128,768]{2,1,0:T(8,128)S(1)}, f32[3,128,768]{2,1,0:T(8,128)}, u32[]{:S(2)}) copy-start(f32[3,128,768]{2,1,0:T(8,128)} %get-tuple-element.8) | copy-start | bytes 3538948

commit v6 on v5

--- a/solution.py
+++ b/solution.py
@@ -431,7 +431,7 @@
         def _():
             pass_on(tick)
 
-        @pl.when((tick >= parts) & (tick < chunks - parts))
+        @pl.when((tick > 0) & (tick < chunks - parts))
         def _():
             send_own(tick + parts)
 
@@ -463,7 +463,9 @@
             def _(h):
                 reverse(tick * group + h)
 
-            send_own(tick + parts)
+        @pl.when(tick == 0)
+        def _():
+            send_own(parts)
 
         @pl.when(tick < chunks)
         def _():

time: 101 us -> 100 us (0.990)
  no operation moved by 1% of the time
where the time goes in v6:
time: 100 us
  Pallas kernels  94.8 us (95%)
  local copies, waits for them, and re-layouts  4.76 us (5%)
    pallas_call x1, Pallas kernels, layer(): pl.pallas_call(functools.partial(layer_kernel, n_dp, n_seq, n_head), out_...  94.8 us
    unnamed x5, local copies, waits for them, and re-layouts  4.76 us

profile of v6, /device:TPU:0, one launch (start us, length us, event | category | flops | bytes accessed | tf_op | source)
XLA Modules:
  0.0 100.2 jit_solution(14431721830561828302)
XLA Ops:
  0.6 94.8 %layer.1 = (bf16[256,768]{1,0:T(8,128)(2,1)}, f32[3,128,768]{2,1,0:T(8,128)}, bf16[128,2048]{1,0:T(8,128)(2,1)}) custom-call(bf16[256,2048]{1,0:T(8,128)(2,1)} %bitcast.10, bf16[3,2048,768]{2,1,0:T(8,128)(2,1)} %bitcast.8, f32[1,128]{1,0:T(1,128)} %bitcast.14, f32[1,128]{1,0:T(1,128)} %bitcast.15, s32[16,9]{1,0:T(8,128)} %near_ref.1, bf16[256,768]{1,0:T(8,128)(2,1)} %bitcast.12), custom_call_target="tpu_custom_call" | custom-call | tf_op jit(solution)/shard_map/layer/pallas_call | solution.py:543
  95.5 0.0 copy-start
  95.5 1.9 %copy.12 = bf16[1,256,768]{2,1,0:T(8,128)(2,1)} copy(bf16[1,256,768]{2,1,0:T(8,128)(2,1)} %bitcast.13) | data formatting | bytes 786432
  97.4 1.9 %copy.13 = bf16[1,128,2048]{2,1,0:T(8,128)(2,1)} copy(bf16[1,128,2048]{2,1,0:T(8,128)(2,1)} %bitcast.11) | data formatting | bytes 1048576
  99.2 0.0 copy-done
  99.2 1.0 %copy.14 = f32[128,3,768]{2,0,1:T(8,128)} copy(f32[128,3,768]{2,0,1:T(8,128)S(1)} %bitcast.9) | data formatting | bytes 2359296
Async XLA Ops:
  95.5 3.8 %copy-start = (f32[3,128,768]{2,1,0:T(8,128)S(1)}, f32[3,128,768]{2,1,0:T(8,128)}, u32[]{:S(2)}) copy-start(f32[3,128,768]{2,1,0:T(8,128)} %get-tuple-element.8) | copy-start | bytes 3538948
